TPU v7x, 32 devices: a whole 2x2x4 slice. The times are simulated.
32 devices in a mesh: inst: 2 (over core), lon: 16 (over z, y, x).
Axes of the slice: x: 2, y: 2, z: 4, core: 2. Of those that a mesh axis runs over, the one named last changes fastest.
Arguments:
- obs_x: bfloat16 [384, 128, 256], P(('inst', 'lon')), may hold values from -6 to 6
- obs_cot: bfloat16 [384, 128, 256], P(('inst', 'lon')), may hold values from -6 to 6
- tile_window: int32 [384, 2], P(('inst', 'lon')), may hold values from 0 to 179, as said below
- point_mask: int32 [384, 128], P(('inst', 'lon')), may hold values from 0 to 1, as said below
- band_counts: int32 [32], P(('inst', 'lon')), may hold values from 1 to 12, as said below
- latents: bfloat16 [64, 184, 256], P('lon'), may hold values from -6 to 6
- w_query: bfloat16 [256, 128], replicated, may hold values from -3 to 3
- w_key: bfloat16 [256, 128], replicated, may hold values from -0.375 to 0.375
- w_value: bfloat16 [256, 128], replicated, may hold values from -0.375 to 0.375
- w_out: bfloat16 [128, 256], replicated, may hold values from -0.5 to 0.5
Outputs:
- decoded: bfloat16 [384, 128, 256], P(('inst', 'lon'))
- obs_grad: bfloat16 [384, 128, 256], P(('inst', 'lon'))
- latent_grad: float32 [64, 184, 256], P('lon')
- query_grad: float32 [256, 128], replicated
- key_grad: float32 [256, 128], replicated
- value_grad: float32 [256, 128], replicated
- out_grad: float32 [128, 256], replicated
Inputs may be any that keep to these rules, and one draw needn't show every extreme that they name: `tile_window`: column 0 is the first longitude column of the tile's window; the window's centre column (column 2) mod 64 is one of the 4 columns of the band that holds the tile. Column 1 is the window's first latitude row, at most 179. `point_mask`: in each tile the live slots come first, and half or more of the slots are live. `band_counts`: one entry equals 12.
All inputs are finite; a program needn't handle non-finite values.
Results may differ from a plain program's by a relative error of at most 0.007.
The roundings to bfloat16 on the way count: a program that leaves them out, or rounds other values in their place, can miss the bound.
Values may be sent and summed in bfloat16 or wider, within the bound.
A program may use at most 64 MiB of HBM per device.

v0:
```python
import math

import jax
import jax.numpy as jnp
from jax import lax
from jax.sharding import PartitionSpec as P

HEADS = 4
REACH = 2


softcap = 30.0


def with_halo(block, sides, width):
    for axis, dim in sides:
        count = lax.axis_size(axis)
        forward = [(i, i + 1) for i in range(count - 1)]
        forward.append((count - 1, 0))
        backward = [(target, source) for source, target in forward]
        low = lax.ppermute(
            lax.slice_in_dim(block, block.shape[dim] - width, None, axis=dim), axis, forward
        )
        high = lax.ppermute(lax.slice_in_dim(block, 0, width, axis=dim), axis, backward)
        block = jnp.concatenate([low, block, high], axis=dim)
    return block


def passed_along(block, axis, distance):
    devices = range(lax.axis_size(axis))
    route = [((i - distance) % len(devices), i) for i in devices]
    return lax.ppermute(block, axis, route)


def split_products(grad, w_pair, flat_latents):
    grad_high = grad.astype(jnp.bfloat16)
    grad_low = (grad - grad_high.astype(jnp.float32)).astype(jnp.bfloat16)
    by_rows = (((1,), (1,)), ((), ()))
    by_cols = (((0,), (0,)), ((), ()))
    latent_part = lax.dot_general(
        grad_high, w_pair, by_rows, preferred_element_type=jnp.float32
    ) + lax.dot_general(grad_low, w_pair, by_rows, preferred_element_type=jnp.float32)
    pair_weight = lax.dot_general(
        flat_latents, grad_high, by_cols, preferred_element_type=jnp.float32
    ) + lax.dot_general(flat_latents, grad_low, by_cols, preferred_element_type=jnp.float32)
    return (latent_part, pair_weight)


def attend(obs_x, obs_cot, live_points, windows, w_query, w_out):
    n_tiles, tile_len, model_width = obs_x.shape
    attn_width = w_query.shape[1]
    head_size = attn_width // HEADS
    score_scale = 1.0 / math.sqrt(head_size)
    flat_x = obs_x.reshape(-1, model_width)
    queries = jnp.dot(flat_x, w_query, preferred_element_type=jnp.float32).astype(jnp.bfloat16)
    query_heads = queries.reshape(n_tiles, tile_len, HEADS, head_size)
    win_keys = windows[:, :, :attn_width].reshape(n_tiles, -1, HEADS, head_size)
    win_values = windows[:, :, attn_width:].reshape(n_tiles, -1, HEADS, head_size)
    raw_scores = (
        jnp.einsum("nqhd,nkhd->nhqk", query_heads, win_keys, preferred_element_type=jnp.float32)
        * score_scale
    )
    capped = softcap * jnp.tanh(raw_scores / softcap)
    weights = jnp.exp(capped)
    probs = weights / jnp.sum(weights, axis=-1, keepdims=True)
    probs_b = probs.astype(jnp.bfloat16)
    attended = jnp.einsum(
        "nhqk,nkhd->nqhd", probs_b, win_values, preferred_element_type=jnp.float32
    )
    attended = attended.astype(jnp.bfloat16).reshape(-1, attn_width)
    projected = jnp.dot(attended, w_out, preferred_element_type=jnp.float32).reshape(
        n_tiles, tile_len, model_width
    )
    decoded = (obs_x.astype(jnp.float32) + live_points[:, :, None] * projected).astype(jnp.bfloat16)
    masked = obs_cot * live_points.astype(jnp.bfloat16)[:, :, None]
    flat_cot = masked.reshape(-1, model_width)
    out_grad = jnp.dot(attended.T, flat_cot, preferred_element_type=jnp.float32)
    attended_grad = jnp.dot(flat_cot, w_out.T, preferred_element_type=jnp.float32).astype(
        jnp.bfloat16
    )
    attended_grad = attended_grad.reshape(n_tiles, tile_len, HEADS, head_size)
    prob_grad = jnp.einsum(
        "nqhd,nkhd->nhqk", attended_grad, win_values, preferred_element_type=jnp.float32
    )
    row_inner = jnp.sum(probs * prob_grad, axis=-1, keepdims=True)
    score_grad = (
        probs * (prob_grad - row_inner) * (1.0 - (capped / softcap) ** 2) * score_scale
    ).astype(jnp.bfloat16)
    query_part = jnp.einsum(
        "nhqk,nkhd->nqhd", score_grad, win_keys, preferred_element_type=jnp.float32
    )
    query_part = query_part.astype(jnp.bfloat16).reshape(-1, attn_width)
    key_part = jnp.einsum(
        "nhqk,nqhd->nkhd", score_grad, query_heads, preferred_element_type=jnp.float32
    )
    value_part = jnp.einsum(
        "nhqk,nqhd->nkhd", probs_b, attended_grad, preferred_element_type=jnp.float32
    )
    window_grad = jnp.concatenate(
        [key_part.reshape(n_tiles, -1, attn_width), value_part.reshape(n_tiles, -1, attn_width)],
        axis=-1,
    )
    obs_grad = obs_cot.astype(jnp.float32).reshape(-1, model_width) + jnp.dot(
        query_part, w_query.T, preferred_element_type=jnp.float32
    )
    obs_grad = obs_grad.astype(jnp.bfloat16).reshape(n_tiles, tile_len, model_width)
    query_grad = jnp.dot(flat_x.T, query_part, preferred_element_type=jnp.float32)
    return (decoded, obs_grad, window_grad, query_grad, out_grad)


def shards(
    obs_x, obs_cot, tile_window, point_mask, band_counts, latents, w_query, w_key, w_value, w_out
):
    band_cols, lat_rows, model_width = latents.shape
    attn_width = w_query.shape[1]
    lon_cols = band_cols * lax.axis_size("lon")
    window = 2 * REACH + 1
    w_pair = jnp.concatenate([w_key, w_value], axis=1)
    own_pairs = jnp.dot(
        latents.reshape(-1, model_width), w_pair, preferred_element_type=jnp.float32
    ).astype(jnp.bfloat16)
    own_pairs = own_pairs.reshape(band_cols, lat_rows, 2 * attn_width)
    wide_pairs = with_halo(own_pairs, (("lon", 0),), REACH).reshape(-1, 2 * attn_width)
    band_first = lax.axis_index("lon") * band_cols
    offsets = jnp.arange(window, dtype=jnp.int32)
    starts = (tile_window[:, 0:1] - band_first + REACH) % lon_cols + offsets[None, :]
    lat_index = tile_window[:, 1:2] + offsets[None, :]
    key_index = (starts[:, :, None] * lat_rows + lat_index[:, None, :]).reshape(-1, window * window)
    windows = jnp.take(wide_pairs, key_index, axis=0)
    local_tile = jnp.arange(obs_x.shape[0], dtype=jnp.int32)
    live_points = (
        point_mask.astype(jnp.float32) * (local_tile < band_counts[0]).astype(jnp.float32)[:, None]
    )
    decoded, obs_grad, window_grad, query_grad, out_grad = attend(
        obs_x, obs_cot, live_points, windows, w_query, w_out
    )
    wide_cols = band_cols + 2 * REACH
    pair_grad = jnp.zeros((wide_cols * lat_rows, 2 * attn_width), jnp.float32)
    pair_grad = pair_grad.at[key_index.reshape(-1)].add(window_grad.reshape(-1, 2 * attn_width))
    pair_grad = pair_grad.reshape(wide_cols, lat_rows, 2 * attn_width)
    from_right = passed_along(pair_grad[:REACH].astype(jnp.bfloat16), "lon", -1).astype(jnp.float32)
    from_left = passed_along(pair_grad[band_cols + REACH :].astype(jnp.bfloat16), "lon", 1).astype(
        jnp.float32
    )
    own_grad = pair_grad[REACH : band_cols + REACH]
    own_grad = own_grad.at[:REACH].add(from_left)
    own_grad = own_grad.at[band_cols - REACH :].add(from_right)
    flat_grad = own_grad.reshape(-1, 2 * attn_width)
    flat_latents = latents.reshape(-1, model_width)
    latent_part, pair_weight = split_products(flat_grad, w_pair, flat_latents)
    latent_grad = lax.psum(latent_part, "inst")
    query_grad, out_grad, pair_weight = lax.psum(
        (query_grad, out_grad, pair_weight), ("inst", "lon")
    )
    return (
        decoded,
        obs_grad,
        latent_grad.reshape(band_cols, lat_rows, model_width),
        query_grad,
        pair_weight[:, :attn_width],
        pair_weight[:, attn_width:],
        out_grad,
    )


def solution(mesh):
    placed = (
        P(("inst", "lon"), None, None),
        P(("inst", "lon"), None, None),
        P(("inst", "lon"), None),
        P(("inst", "lon"), None),
        P(("inst", "lon")),
        P("lon", None, None),
        P(),
        P(),
        P(),
        P(),
    )
    return jax.shard_map(
        shards,
        mesh=mesh,
        in_specs=placed,
        out_specs=(
            P(("inst", "lon"), None, None),
            P(("inst", "lon"), None, None),
            P("lon", None, None),
            P(),
            P(),
            P(),
            P(),
        ),
        check_vma=False,
    )
```

profile of v0, /device:TPU:0, one launch (start us, length us, event | category | flops | bytes accessed | tf_op | source)
XLA Modules:
  0.0 227.1 jit_solution(15239581388625097601)
XLA Ops:
  10.1 7.0 %collective-permute-start.1 = (bf16[2,184,256]{2,1,0:T(8,128)(2,1)}, bf16[2,184,256]{2,1,0:T(8,128)(2,1)}, u32[]{:S(2)}, u32[]{:S(2)}) collective-permute-start(bf16[2,184,256]{2,1,0:T(8,128)(2,1)} %bitcast.7), channel_id=1, source_target_pairs={{1,0},{2,1},{3,2},{4,3},{5,4},{6,5},{7,6},{8,7},{9,8},{10,9},{11,1... | collective-permute-start | bytes 565256 | tf_op jit(solution)/shard_map/ppermute | solution.py:24
  19.3 1.1 reshape.270
  21.1 1.4 broadcast_multiply_fusion
  22.5 1.1 convolution_convert_fusion
  23.6 1.2 copy.37
  24.7 1.1 reshape.275
  27.2 1.1 pad_maximum_fusion
  28.3 2.0 gather_fusion
  31.8 1.2 fusion.36
  34.3 1.1 convolution_convert_fusion.3
  35.4 3.2 %fusion.8 = bf16[12,128,4,32]{1,3,2,0:T(8,128)(2,1)} fusion(bf16[12,25,4,32]{1,3,2,0:T(8,128)(2,1)S(1)} %bitcast.118, f32[12,4,128,25]{2,3,1,0:T(8,128)} %fusion.36, f32[12,4,128,25]{2,3,1,0:T(8,128)} %copy-done.23, f32[12,4,128]{2,1,0:T(4,128)S(1)} %get-tuple-element.62), kind=kOutput, calls=%fused_computation.21 | convolution fusion | flops 11876376 | bytes 1723392 | tf_op jit(solution)/shard_map/nhqk,nkhd->nqhd/dot_general | solution.py:89
  38.6 2.7 %convolution_bitcast_fusion.1 = f32[12,25,4,32]{1,3,2,0:T(8,128)S(1)} fusion(f32[12,4,128,25]{2,3,1,0:T(8,128)} %fusion.36, f32[12,4,128,25]{2,3,1,0:T(8,128)} %copy-done.23, bf16[12,128,4,32]{1,0,3,2:T(8,128)(2,1)} %reshape.270, f32[12,4,128]{2,1,0:T(4,128)S(1)} %get-tuple-element.62), kind=kOutput, calls=%fused_computation.12 | convolution fusion | flops 11679768 | bytes 1800192 | tf_op jit(solution)/shard_map/nhqk,nqhd->nkhd/dot_general | solution.py:93
  41.3 2.4 %convolution_bitcast_fusion = f32[12,25,4,32]{1,3,2,0:T(8,128)} fusion(bf16[12,128,4,32]{1,0,3,2:T(8,128)(2,1)S(1)} %copy-done.6, f32[12,4,128,25]{2,3,1,0:T(8,128)} %copy-done.23, f32[12,4,128]{2,1,0:T(4,128)S(1)} %get-tuple-element.62), kind=kOutput, calls=%fused_computation.11 | convolution fusion | flops 10291200 | bytes 1185792 | tf_op jit(solution)/shard_map/nhqk,nqhd->nkhd/dot_general | solution.py:96
  43.6 1.5 copy.45
  47.4 3.0 %scatter_custom_fusion = f32[1472,256]{1,0:T(8,128)S(1)} fusion(s32[300]{0:T(512)} %fusion.45, f32[]{:T(128)} %constant.106.clone.1, f32[300,128]{1,0:T(8,128)} %concatenate.21, f32[]{:T(128)} %constant.116, f32[300,128]{1,0:T(8,128)} %concatenate.20), kind=kCustom, calls=%fused_computation.37 | custom fusion | flops 153600 | bytes 1819648 | tf_op jit(solution)/shard_map/scatter-add | solution.py:139
  53.3 5.6 %collective-permute-start.3 = (bf16[2,184,256]{2,1,0:T(8,128)(2,1)S(1)}, bf16[2,184,256]{2,1,0:T(8,128)(2,1)S(1)}, u32[]{:S(2)}, u32[]{:S(2)}) collective-permute-start(bf16[2,184,256]{2,1,0:T(8,128)(2,1)S(1)} %bitcast.119), channel_id=1, source_target_pairs={{1,0},{2,1},{3,2},{4,3},{5,4},{6,5},{7,6},{8,7},{9,8},{10,9},{11,1... | collective-permute-start | bytes 565256 | tf_op jit(solution)/shard_map/ppermute | solution.py:32
  59.9 2.6 %collective-permute-done.2 = bf16[2,184,256]{2,1,0:T(8,128)(2,1)S(1)} collective-permute-done((bf16[2,184,256]{2,1,0:T(8,128)(2,1)S(1)}, bf16[2,184,256]{2,1,0:T(8,128)(2,1)S(1)}, u32[]{:S(2)}, u32[]{:S(2)}) %collective-permute-start.2) | collective-permute-done | bytes 188448 | tf_op jit(solution)/shard_map/ppermute | solution.py:32
  65.2 2.2 convolution_add_fusion.1
  67.5 1.3 fusion.1
  68.8 1.3 add_convert_fusion
  70.1 126.6 %all-reduce.6.cloned.1.call-done = (f32[256,128]{0,1:T(8,128)}, f32[256,256]{0,1:T(8,128)}, f32[128,256]{1,0:T(8,128)}) async-done(((f32[256,128]{0,1:T(8,128)}, f32[256,256]{0,1:T(8,128)}, f32[128,256]{1,0:T(8,128)}), (f32[256,128]{0,1:T(8,128)}, f32[256,256]{0,1:T(8,128)}, f32[128,256]{1,0:T(8,128)})) %all-reduce.6.cloned.1.call-update) | async-done | bytes 524304 | tf_op jit(solution)/shard_map/psum | solution.py:152
  196.7 1.7 copy.47
  200.9 16.7 %all-reduce.4.cloned.1.call-done = f32[4,184,256]{2,1,0:T(8,128)} async-done(((f32[4,184,256]{2,1,0:T(8,128)}), f32[4,184,256]{2,1,0:T(8,128)}) %all-reduce.4.cloned.1.call-update) | async-done | bytes 753680 | tf_op jit(solution)/shard_map/psum | solution.py:151
  217.6 2.0 copy.87
  (109 shorter events, 21.0 us)
Async XLA Ops:
  7.2 1.9 copy-start
  7.2 9.9 %copy-start.22 = (s32[12,2]{0,1:T(2,128)S(1)}, s32[12,2]{0,1:T(2,128)}, u32[]{:S(2)}) copy-start(s32[12,2]{0,1:T(2,128)} %param.16) | copy-start | bytes 292
  7.2 11.5 %copy-start.15 = (bf16[256,128]{1,0:T(8,128)(2,1)S(1)}, bf16[256,128]{1,0:T(8,128)(2,1)}, u32[]{:S(2)}) copy-start(bf16[256,128]{1,0:T(8,128)(2,1)} %param.20) | copy-start | bytes 196612
  7.2 11.5 %copy-start.2 = (bf16[12,128,256]{2,1,0:T(8,128)(2,1)S(1)}, bf16[12,128,256]{2,1,0:T(8,128)(2,1)}, u32[]{:S(2)}) copy-start(bf16[12,128,256]{2,1,0:T(8,128)(2,1)} %param.14) | copy-start | bytes 2359300
  7.2 189.5 %all-reduce.6.cloned.1.call-start = ((), (), s32[]{:S(2)}) async-start(), calls=%async_computation.1 | async-start | bytes 1048576 | tf_op jit(solution)/shard_map/psum | solution.py:152
  9.1 10.0 %copy-start.7 = (bf16[256,256]{1,0:T(8,128)(2,1)}, bf16[256,256]{1,0:T(8,128)(2,1)S(1)}, u32[]{:S(2)}) copy-start(bf16[256,256]{1,0:T(8,128)(2,1)S(1)} %constant_dynamic-update-slice_fusion) | copy-start | bytes 393220
  10.1 16.3 %collective-permute-start.1 = (bf16[2,184,256]{2,1,0:T(8,128)(2,1)}, bf16[2,184,256]{2,1,0:T(8,128)(2,1)}, u32[]{:S(2)}, u32[]{:S(2)}) collective-permute-start(bf16[2,184,256]{2,1,0:T(8,128)(2,1)} %bitcast.7), channel_id=1, source_target_pairs={{1,0},{2,1},{3,2},{4,3},{5,4},{6,5},{7,6},{8,7},{9,8},{10,9},{11,1... | collective-permute-start | bytes 565256 | tf_op jit(solution)/shard_map/ppermute | solution.py:24
  17.1 10.1 %collective-permute-start = (bf16[2,184,256]{2,1,0:T(8,128)(2,1)}, bf16[2,184,256]{2,1,0:T(8,128)(2,1)}, u32[]{:S(2)}, u32[]{:S(2)}) collective-permute-start(bf16[2,184,256]{2,1,0:T(8,128)(2,1)} %bitcast.5), channel_id=1, source_target_pairs={{0,1},{1,2},{2,3},{3,4},{4,5},{5,6},{6,7},{7,8},{8,9},{9,10},{10,1... | collective-permute-start | bytes 565256 | tf_op jit(solution)/shard_map/ppermute | solution.py:21
  18.5 1.9 copy-start.21
  19.1 3.4 %copy-start.17 = (bf16[128,256]{1,0:T(8,128)(2,1)S(1)}, bf16[128,256]{1,0:T(8,128)(2,1)}, u32[]{:S(2)}) copy-start(bf16[128,256]{1,0:T(8,128)(2,1)} %param.23) | copy-start | bytes 196612
  30.3 1.5 copy-start.6
  30.5 2.5 %copy-start.11 = (bf16[12,128,4,32]{1,0,3,2:T(8,128)(2,1)S(1)}, bf16[12,128,4,32]{1,0,3,2:T(8,128)(2,1)}, u32[]{:S(2)}) copy-start(bf16[12,128,4,32]{1,0,3,2:T(8,128)(2,1)} %reshape.270) | copy-start | bytes 1179652
  50.5 2.4 %copy-start.9 = (bf16[12,4,32,128]{3,2,1,0:T(8,128)(2,1)S(1)}, bf16[12,4,32,128]{3,2,1,0:T(8,128)(2,1)}, u32[]{:S(2)}) copy-start(bf16[12,4,32,128]{3,2,1,0:T(8,128)(2,1)} %convolution_convert_fusion.3) | copy-start | bytes 1179652
  52.0 7.9 %copy-start.3 = (bf16[12,128,4,32]{1,0,3,2:T(8,128)(2,1)}, bf16[12,128,4,32]{1,0,3,2:T(8,128)(2,1)S(1)}, u32[]{:S(2)}) copy-start(bf16[12,128,4,32]{1,0,3,2:T(8,128)(2,1)S(1)} %copy.41) | copy-start | bytes 1179652
  52.9 9.6 %slice-start = ((f32[1472,256]{1,0:T(8,128)}), f32[368,256]{1,0:T(8,128)S(1)}, s32[]{:S(2)}) async-start(f32[1472,256]{1,0:T(8,128)} %copy-done.1), calls=%async_computation.2 | async-start | bytes 753664 | tf_op jit(solution)/shard_map/slice.60
  52.9 9.6 %slice-start.1 = ((f32[1472,256]{1,0:T(8,128)}), f32[736,256]{1,0:T(8,128)S(1)}, s32[]{:S(2)}) async-start(f32[1472,256]{1,0:T(8,128)} %copy-done.1), calls=%async_computation.3 | async-start | bytes 1507328 | tf_op jit(solution)/shard_map/slice | solution.py:145
  53.2 9.2 %collective-permute-start.2 = (bf16[2,184,256]{2,1,0:T(8,128)(2,1)S(1)}, bf16[2,184,256]{2,1,0:T(8,128)(2,1)S(1)}, u32[]{:S(2)}, u32[]{:S(2)}) collective-permute-start(bf16[2,184,256]{2,1,0:T(8,128)(2,1)S(1)} %bitcast.120), channel_id=1, source_target_pairs={{15,0},{0,1},{1,2},{2,3},{3,4},{4,5},{5,6},{6,7},{7,8},{8,9},{9,10... | collective-permute-start | bytes 565256 | tf_op jit(solution)/shard_map/ppermute | solution.py:32
  53.3 9.2 %collective-permute-start.3 = (bf16[2,184,256]{2,1,0:T(8,128)(2,1)S(1)}, bf16[2,184,256]{2,1,0:T(8,128)(2,1)S(1)}, u32[]{:S(2)}, u32[]{:S(2)}) collective-permute-start(bf16[2,184,256]{2,1,0:T(8,128)(2,1)S(1)} %bitcast.119), channel_id=1, source_target_pairs={{1,0},{2,1},{3,2},{4,3},{5,4},{6,5},{7,6},{8,7},{9,8},{10,9},{11,1... | collective-permute-start | bytes 565256 | tf_op jit(solution)/shard_map/ppermute | solution.py:32
  62.9 1.8 copy-start.8
  65.1 2.4 %copy-start.4 = (bf16[12,128,4,32]{1,0,3,2:T(8,128)(2,1)S(1)}, bf16[12,128,4,32]{1,0,3,2:T(8,128)(2,1)}, u32[]{:S(2)}) copy-start(bf16[12,128,4,32]{1,0,3,2:T(8,128)(2,1)} %copy-done.3) | copy-start | bytes 1179652
  65.1 2.4 %copy-start.5 = (bf16[12,128,256]{2,1,0:T(8,128)(2,1)S(1)}, bf16[12,128,256]{2,1,0:T(8,128)(2,1)}, u32[]{:S(2)}) copy-start(bf16[12,128,256]{2,1,0:T(8,128)(2,1)} %param.15) | copy-start | bytes 2359300
  65.1 2.4 %copy-start.16 = (bf16[256,128]{1,0:T(8,128)(2,1)S(1)}, bf16[256,128]{1,0:T(8,128)(2,1)}, u32[]{:S(2)}) copy-start(bf16[256,128]{1,0:T(8,128)(2,1)} %param.20) | copy-start | bytes 196612
  65.1 152.5 %all-reduce.4.cloned.1.call-start = ((), (), s32[]{:S(2)}) async-start(), calls=%async_computation | async-start | bytes 1507328 | tf_op jit(solution)/shard_map/psum | solution.py:151
  196.7 23.0 %copy-start.19 = (f32[128,256]{1,0:T(8,128)S(1)}, f32[128,256]{1,0:T(8,128)}, u32[]{:S(2)}) copy-start(f32[128,256]{1,0:T(8,128)} %get-tuple-element.72) | copy-start | bytes 393220
  (8 other events, 9.6 us)
Sparse Core Ops, SparseCore 0:
  65.2 131.4 all-reduce.5
  199.6 17.9 all-reduce.3
where the time goes:
time: 228 us; the launch traced here: 227 us
  waiting for transfers between devices  147 us (64%)
  local copies, waits for them, and re-layouts  23.6 us (10%)
  matrix products  21 us (9%)
  between operations  15.1 us (7%)
  starting transfers between devices  12.7 us (6%)
  other arithmetic  8.08 us (4%)
    psum x1, waiting for transfers between devices, shards(): lax.psum((query_grad, out_grad, pair_weight), ('inst', 'lon'))  127 us
    psum x1, waiting for transfers between devices, shards(): latent_grad = lax.psum(latent_part, 'inst')  16.7 us
    unnamed x54, local copies, waits for them, and re-layouts  9 us
    ppermute x1, starting transfers between devices, with_halo(): lax.ppermute(lax.slice_in_dim(block, 0, width, axis=dim), axis, backward)  6.97 us
    ppermute x2, starting transfers between devices, passed_along(): return lax.ppermute(block, axis, route)  5.67 us
  transfers between devices with their start and end apart: 6, of which 4 were waited for; matrix products, arithmetic and copies ran while one was open for 8% of the time, Pallas kernels for 0%

commit v1 on v0

v1 whole, which is shorter than its diff:
```python
import functools
import math

import jax
import jax.numpy as jnp
from jax import lax
from jax.experimental import pallas as pl
from jax.experimental.pallas import tpu as pltpu
from jax.sharding import PartitionSpec as P

HEADS = 4
REACH = 2
WINDOW = 2 * REACH + 1
SUB = 8
CAP = 30.0
MESH = pl.DeviceIdType.MESH
F32 = jnp.float32
BF16 = jnp.bfloat16

NT = (((1,), (1,)), ((), ()))
TN = (((0,), (0,)), ((), ()))


def dot(a, b, dims=(((1,), (0,)), ((), ()))):
    return lax.dot_general(a, b, dims, preferred_element_type=F32)


def halo_kernel(n_lon, lat, low, high, send, recv):
    me = lax.axis_index("lon")
    right, left = lax.rem(me + 1, n_lon), lax.rem(me + n_lon - 1, n_lon)
    barrier = pltpu.get_barrier_semaphore()
    for other in (left, right):
        pl.semaphore_signal(barrier, inc=1, device_id={"lon": other}, device_id_type=MESH)
    pl.semaphore_wait(barrier, 2)
    edge = low.shape[0]
    rows = lat.shape[0]
    up = pltpu.make_async_remote_copy(
        src_ref=lat.at[pl.ds(rows - edge, edge)], dst_ref=low, send_sem=send.at[0],
        recv_sem=recv.at[0], device_id={"lon": right}, device_id_type=MESH)
    down = pltpu.make_async_remote_copy(
        src_ref=lat.at[pl.ds(0, edge)], dst_ref=high, send_sem=send.at[1],
        recv_sem=recv.at[1], device_id={"lon": left}, device_id_type=MESH)
    up.start()
    down.start()
    up.wait()
    down.wait()


def attend_kernel(
    lon_cols, lat_rows, tw, cnt, x_ref, cot_ref, mask_ref, lat, low, high, wq, wk, wv, wo,
    dec, og, own_out, halo_out, g_out, keys, values, kg, vg, qg, outg,
):
    step = pl.program_id(0)
    tiles, length, width = x_ref.shape
    attn = wq.shape[1]
    head = attn // HEADS
    scale = 1.0 / math.sqrt(head)
    own_rows, edge = lat.shape[0], low.shape[0]
    wide = own_rows + 2 * edge
    slots = WINDOW * SUB
    band_cols = own_rows // lat_rows

    @pl.when(step == 0)
    def _():
        w_pair = jnp.concatenate([wk[...], wv[...]], axis=1)

        def project(block):
            return dot(block[...], w_pair).astype(BF16).astype(F32)

        for ref, first, count in ((low, 0, edge), (lat, edge, own_rows), (high, edge + own_rows, edge)):
            block = project(ref)
            keys[pl.ds(first, count), :] = block[:, :attn]
            values[pl.ds(first, count), :] = block[:, attn:]
        keys[pl.ds(wide, SUB), :] = jnp.zeros((SUB, attn), F32)
        values[pl.ds(wide, SUB), :] = jnp.zeros((SUB, attn), F32)
        kg[...] = jnp.zeros_like(kg)
        vg[...] = jnp.zeros_like(vg)
        qg[...] = jnp.zeros_like(qg)
        outg[...] = jnp.zeros_like(outg)

    flat_x = x_ref[...].reshape(tiles * length, width)
    flat_cot = cot_ref[...].reshape(tiles * length, width)
    queries = dot(flat_x, wq[...]).astype(BF16)

    row_id = lax.broadcasted_iota(jnp.int32, (length, width), 0)
    lives = []
    for j in range(tiles):
        t = step * tiles + j
        used = jnp.sum(mask_ref[pl.ds(t, 1), :], axis=1, keepdims=True)
        used = jnp.where(t < cnt[0], used, 0)
        lives.append(row_id < used)
    live = jnp.concatenate([m.astype(F32) for m in lives], axis=0)
    masked = (flat_cot.astype(F32) * live).astype(BF16)
    att_grad = dot(masked, wo[...], NT).astype(BF16)

    lane = lax.broadcasted_iota(jnp.int32, (1, attn), 1) // head
    head_mask = [(lane == h).astype(F32) for h in range(HEADS)]
    slot_id = lax.broadcasted_iota(jnp.int32, (slots, length), 0)
    valid = ((slot_id & (SUB - 1)) < WINDOW)[None]
    band_first = lax.axis_index("lon") * band_cols

    att_parts, query_parts = [], []
    for j in range(tiles):
        t = step * tiles + j
        col = lax.rem(tw[t, 0] - band_first + REACH + lon_cols, lon_cols)
        base = col * lat_rows + tw[t, 1]
        q_t = queries[j * length : (j + 1) * length]
        g_t = att_grad[j * length : (j + 1) * length]
        spans = [pl.ds(base + a * lat_rows, SUB) for a in range(WINDOW)]
        kw = jnp.concatenate([keys[at, :] for at in spans], axis=0)
        vw = jnp.concatenate([values[at, :] for at in spans], axis=0)
        kb = jnp.concatenate([kw * m for m in head_mask], axis=0).astype(BF16)
        vb = jnp.concatenate([vw * m for m in head_mask], axis=0).astype(BF16)
        th = jnp.tanh(dot(kb, q_t, NT) * scale / CAP).reshape(HEADS, slots, length)
        e = jnp.where(valid, jnp.exp(CAP * th), 0.0)
        p = e * (1.0 / jnp.sum(e, axis=1, keepdims=True))
        dp = dot(vb, g_t, NT).reshape(HEADS, slots, length)
        inner = jnp.sum(p * dp, axis=1, keepdims=True)
        sg = p * (dp - inner) * (1.0 - th * th) * scale
        sg = sg.reshape(HEADS * slots, length).astype(BF16)
        pb = p.reshape(HEADS * slots, length).astype(BF16)
        att_parts.append(dot(pb, vb, TN).astype(BF16))
        query_parts.append(dot(sg, kb, TN).astype(BF16))
        kp = dot(sg, q_t)
        vp = dot(pb, g_t)
        k_sum = sum(kp[h * slots : (h + 1) * slots] * head_mask[h] for h in range(HEADS))
        v_sum = sum(vp[h * slots : (h + 1) * slots] * head_mask[h] for h in range(HEADS))
        for a, at in enumerate(spans):
            kg[at, :] = kg[at, :] + k_sum[a * SUB : (a + 1) * SUB]
            vg[at, :] = vg[at, :] + v_sum[a * SUB : (a + 1) * SUB]

    attended = jnp.concatenate(att_parts, axis=0)
    query_part = jnp.concatenate(query_parts, axis=0)
    dec[...] = (flat_x.astype(F32) + live * dot(attended, wo[...])).astype(BF16).reshape(dec.shape)
    og[...] = (flat_cot.astype(F32) + dot(query_part, wq[...], NT)).astype(BF16).reshape(og.shape)
    qg[...] += dot(flat_x, query_part, TN)
    outg[...] += dot(attended, masked, TN)

    @pl.when(step == pl.num_programs(0) - 1)
    def _():
        for ref, lanes in ((kg, pl.ds(0, attn)), (vg, pl.ds(attn, attn))):
            own_out[:, lanes] = ref[pl.ds(edge, own_rows), :]
            halo_out[pl.ds(0, edge), lanes] = ref[pl.ds(0, edge), :].astype(BF16)
            halo_out[pl.ds(edge, edge), lanes] = ref[pl.ds(edge + own_rows, edge), :].astype(BF16)
        kv = jnp.zeros((width, 2 * attn), F32)
        for ref, first, count in ((low, 0, edge), (lat, edge, own_rows), (high, edge + own_rows, edge)):
            rows_at = pl.ds(first, count)
            grad = jnp.concatenate([kg[rows_at, :], vg[rows_at, :]], axis=1)
            grad_high = grad.astype(BF16)
            grad_low = (grad - grad_high.astype(F32)).astype(BF16)
            kv = kv + dot(ref[...], grad_high, TN) + dot(ref[...], grad_low, TN)
        rows = g_out.shape[1]
        pieces = (qg[...], kv[:, :attn], kv[:, attn:], outg[:, :attn], outg[:, attn:])
        at = 0
        for piece in pieces:
            count = piece.shape[0] // rows
            g_out[pl.ds(at, count)] = piece.astype(BF16).reshape(count, rows, attn)
            at += count


def reduce_kernel(
    n_inst, n_lon, own, halo, g, wk, wv, lat_out, q_out, k_out, v_out, o_out,
    hbuf, shares, rs, part, ag, h_s, h_r, i_s, i_r, rs_s, rs_r, p_s, p_r, a_s, a_r,
):
    me, mi = lax.axis_index("lon"), lax.axis_index("inst")
    edge = hbuf.shape[1]
    own_rows = own.shape[0]
    attn = wk.shape[1]

    def lon_at(d):
        return lax.rem(me + d, n_lon)

    def inst_at(d):
        return lax.rem(mi + d, n_inst)

    barrier = pltpu.get_barrier_semaphore()
    for d in range(1, n_lon):
        pl.semaphore_signal(barrier, inc=1, device_id={"lon": lon_at(d)}, device_id_type=MESH)
    for d in range(1, n_inst):
        pl.semaphore_signal(barrier, inc=1, device_id={"inst": inst_at(d)}, device_id_type=MESH)
    pl.semaphore_wait(barrier, n_lon + n_inst - 2)

    def send(src, dst, s, r, target):
        copy = pltpu.make_async_remote_copy(
            src_ref=src, dst_ref=dst, send_sem=s, recv_sem=r, device_id=target,
            device_id_type=MESH)
        copy.start()
        return copy

    halos = [
        send(halo.at[pl.ds(0, edge)], hbuf.at[0], h_s.at[0], h_r.at[0], {"lon": lon_at(n_lon - 1)}),
        send(halo.at[pl.ds(edge, edge)], hbuf.at[1], h_s.at[1], h_r.at[1], {"lon": lon_at(1)}),
    ]
    scatters = [
        send(g.at[lon_at(d)], rs.at[d], rs_s.at[d], rs_r.at[d], {"lon": lon_at(d)})
        for d in range(1, n_lon)
    ]
    for copy in scatters:
        copy.wait()
    total = g[me].astype(F32)
    for d in range(1, n_lon):
        total = total + rs[d].astype(F32)
    part[mi] = total
    swaps = [
        send(part.at[mi], part.at[mi], p_s.at[d], p_r.at[d], {"inst": inst_at(d)})
        for d in range(1, n_inst)
    ]
    for copy in halos:
        copy.wait()
    shares[mi, pl.ds(0, edge), :] = (own[pl.ds(0, edge), :] + hbuf[1].astype(F32)).astype(BF16)
    shares[mi, pl.ds(own_rows - edge, edge), :] = (
        own[pl.ds(own_rows - edge, edge), :] + hbuf[0].astype(F32)
    ).astype(BF16)
    joins = [
        send(shares.at[mi], shares.at[mi], i_s.at[d], i_r.at[d], {"inst": inst_at(d)})
        for d in range(1, n_inst)
    ]
    for copy in swaps:
        copy.wait()
    total = part[0]
    for i in range(1, n_inst):
        total = total + part[i]
    ag[me] = total.astype(BF16)
    gathers = [
        send(ag.at[me], ag.at[me], a_s.at[d], a_r.at[d], {"lon": lon_at(d)})
        for d in range(1, n_lon)
    ]
    for copy in joins:
        copy.wait()
    grad = shares[0].astype(F32)
    for i in range(1, n_inst):
        grad = grad + shares[i].astype(F32)
    grad_high = grad.astype(BF16)
    grad_low = (grad - grad_high.astype(F32)).astype(BF16)
    w_pair = jnp.concatenate([wk[...], wv[...]], axis=1)
    lat_out[...] = dot(grad_high, w_pair, NT) + dot(grad_low, w_pair, NT)
    for copy in gathers:
        copy.wait()
    rows = ag.shape[1]
    at = 0

    def take(count):
        nonlocal at
        block = ag[pl.ds(at, count // rows)].astype(F32).reshape(count, attn)
        at += count // rows
        return block

    q_out[...] = take(q_out.shape[0])
    k_out[...] = take(k_out.shape[0])
    v_out[...] = take(v_out.shape[0])
    o_out[:, pl.ds(0, attn)] = take(o_out.shape[0])
    o_out[:, pl.ds(attn, attn)] = take(o_out.shape[0])


def vmem():
    return pl.BlockSpec(memory_space=pltpu.VMEM)


def shards(
    n_inst, n_lon, obs_x, obs_cot, tile_window, point_mask, band_counts, latents,
    w_query, w_key, w_value, w_out,
):
    n_tiles, length, width = obs_x.shape
    band_cols, lat_rows, _ = latents.shape
    attn = w_query.shape[1]
    edge, own_rows = REACH * lat_rows, band_cols * lat_rows
    wide = own_rows + 2 * edge
    flat = latents.reshape(own_rows, width)
    dma = pltpu.SemaphoreType.DMA
    low, high = pl.pallas_call(
        functools.partial(halo_kernel, n_lon),
        out_shape=[jax.ShapeDtypeStruct((edge, width), BF16)] * 2,
        in_specs=[pl.BlockSpec(memory_space=pl.ANY)],
        out_specs=[pl.BlockSpec(memory_space=pl.ANY)] * 2,
        scratch_shapes=[dma((2,)), dma((2,))],
        compiler_params=pltpu.CompilerParams(collective_id=0, has_side_effects=True),
        name="halo",
    )(flat)

    group = next(b for b in (4, 3, 2, 1) if n_tiles % b == 0)
    weight_rows = 2 * width + 2 * attn + width
    rows = weight_rows // n_lon
    whole = lambda *shape: pl.BlockSpec(shape, lambda i: (0,) * len(shape))
    tile_spec = pl.BlockSpec((group, length, width), lambda i: (i, 0, 0))
    smem = pl.BlockSpec(memory_space=pltpu.SMEM)
    decoded, obs_grad, own, halo, g = pl.pallas_call(
        functools.partial(attend_kernel, band_cols * n_lon, lat_rows),
        grid=(n_tiles // group,),
        out_shape=[
            jax.ShapeDtypeStruct(obs_x.shape, BF16),
            jax.ShapeDtypeStruct(obs_x.shape, BF16),
            jax.ShapeDtypeStruct((own_rows, 2 * attn), F32),
            jax.ShapeDtypeStruct((2 * edge, 2 * attn), BF16),
            jax.ShapeDtypeStruct((n_lon, rows, attn), BF16),
        ],
        in_specs=[
            smem, smem, tile_spec, tile_spec, whole(n_tiles, length), whole(own_rows, width),
            whole(edge, width), whole(edge, width), whole(width, attn), whole(width, attn),
            whole(width, attn), whole(attn, width),
        ],
        out_specs=[
            tile_spec, tile_spec, whole(own_rows, 2 * attn), whole(2 * edge, 2 * attn),
            whole(n_lon, rows, attn),
        ],
        scratch_shapes=[
            pltpu.VMEM((wide + SUB, attn), F32),
            pltpu.VMEM((wide + SUB, attn), F32),
            pltpu.VMEM((wide + SUB, attn), F32),
            pltpu.VMEM((wide + SUB, attn), F32),
            pltpu.VMEM((width, attn), F32),
            pltpu.VMEM((attn, width), F32),
        ],
        name="attend",
    )(tile_window, band_counts, obs_x, obs_cot, point_mask, flat, low, high,
      w_query, w_key, w_value, w_out)

    latent_grad, query_grad, key_grad, value_grad, out_grad = pl.pallas_call(
        functools.partial(reduce_kernel, n_inst, n_lon),
        out_shape=[
            jax.ShapeDtypeStruct((own_rows, width), F32),
            jax.ShapeDtypeStruct((width, attn), F32),
            jax.ShapeDtypeStruct((width, attn), F32),
            jax.ShapeDtypeStruct((width, attn), F32),
            jax.ShapeDtypeStruct((attn, width), F32),
        ],
        in_specs=[vmem()] * 5,
        out_specs=[vmem()] * 5,
        scratch_shapes=[
            pltpu.VMEM((2, edge, 2 * attn), BF16),
            pltpu.VMEM((n_inst, own_rows, 2 * attn), BF16),
            pltpu.VMEM((n_lon, rows, attn), BF16),
            pltpu.VMEM((n_inst, rows, attn), F32),
            pltpu.VMEM((n_lon, rows, attn), BF16),
            dma((2,)), dma((2,)),
            dma((n_inst,)), dma((n_inst,)),
            dma((n_lon,)), dma((n_lon,)),
            dma((n_inst,)), dma((n_inst,)),
            dma((n_lon,)), dma((n_lon,)),
        ],
        compiler_params=pltpu.CompilerParams(collective_id=1, has_side_effects=True),
        name="reduce",
    )(own, halo, g, w_key, w_value)
    return (
        decoded,
        obs_grad,
        latent_grad.reshape(band_cols, lat_rows, width),
        query_grad,
        key_grad,
        value_grad,
        out_grad,
    )


def solution(mesh):
    placed = (
        P(("inst", "lon"), None, None),
        P(("inst", "lon"), None, None),
        P(("inst", "lon"), None),
        P(("inst", "lon"), None),
        P(("inst", "lon")),
        P("lon", None, None),
        P(),
        P(),
        P(),
        P(),
    )
    return jax.shard_map(
        functools.partial(shards, mesh.shape["inst"], mesh.shape["lon"]),
        mesh=mesh,
        in_specs=placed,
        out_specs=(
            P(("inst", "lon"), None, None),
            P(("inst", "lon"), None, None),
            P("lon", None, None),
            P(),
            P(),
            P(),
            P(),
        ),
        check_vma=False,
    )
```

time: 228 us -> 57.9 us (0.25)
  waiting for transfers between devices: 147 us -> 0 us
  Pallas kernels: 0 us -> 49.4 us
  matrix products: 21 us -> 0 us
  local copies, waits for them, and re-layouts: 23.6 us -> 6.94 us
  between operations: 15.1 us -> 1.32 us
  starting transfers between devices: 12.7 us -> 0 us
  other arithmetic: 8.08 us -> 0 us
    psum x2 -> x0, waiting for transfers between devices: 143 us -> none  [the longest x1 127 us: shards(): lax.psum((query_grad, out_grad, pair_weight), ('inst', 'lon'))]
    pallas_call x0 -> x3, Pallas kernels: none -> 49.4 us  [the longest x1 26.8 us: shards(): pl.pallas_call(functools.partial(reduce_kernel, n_inst, n_lon), out_shape...]
    dot_general x17 -> x0, matrix products: 21 us -> none  [the longest x1 3.19 us: attend(): jnp.einsum('nhqk,nkhd->nqhd', score_grad, win_keys, preferred_element_typ...]
    ppermute x4 -> x0, starting transfers between devices: 12.6 us -> none  [the longest x1 6.97 us: with_halo(): lax.ppermute(lax.slice_in_dim(block, 0, width, axis=dim), axis, backward)]
    ppermute x4 -> x0, waiting for transfers between devices: 3.37 us -> none  [the longest x2 2.63 us: passed_along(): return lax.ppermute(block, axis, route)]
    scatter-add x3 -> x0, other arithmetic: 3.13 us -> none  [the longest x1 3.01 us: shards(): pair_grad.at[key_index.reshape(-1)]]
    reshape x3 -> x0, local copies, waits for them, and re-layouts: 3.12 us -> none  [the longest x1 1.07 us: attend(): query_heads = queries.reshape(n_tiles, tile_len, HEADS, head_size)]
    concatenate x3 -> x0, local copies, waits for them, and re-layouts: 2.79 us -> none  [the longest x2 1.93 us: attend(): jnp.concatenate([key_part.reshape(n_tiles, -1, attn_width), value_part.re...]
  transfers between devices with their start and end apart: 6 -> 0, of which waited for: 4 -> 0; matrix products, arithmetic and copies ran while one was open for 8% -> 0% of each run, Pallas kernels for 0% -> 0%
where the time goes in v1:
time: 57.9 us; the launch traced here: 57.6 us
  Pallas kernels  49.4 us (85%)
  local copies, waits for them, and re-layouts  6.94 us (12%)
  between operations  1.32 us (2%)
    pallas_call x1, Pallas kernels, shards(): pl.pallas_call(functools.partial(reduce_kernel, n_inst, n_lon), out_shape...  26.8 us
    pallas_call x1, Pallas kernels, shards(): pl.pallas_call(functools.partial(halo_kernel, n_lon), out_shape=[jax.Shap...  13.3 us
    pallas_call x1, Pallas kernels, shards(): pl.pallas_call(functools.partial(attend_kernel, band_cols * n_lon, lat_ro...  9.24 us
    unnamed x16, local copies, waits for them, and re-layouts  6.94 us

profile of v1, /device:TPU:0, one launch (start us, length us, event | category | flops | bytes accessed | tf_op | source)
XLA Modules:
  0.0 57.6 jit_solution(14861083125358525872)
XLA Ops:
  1.3 0.0 copy-start.4
  1.3 0.7 %copy-done.4 = s32[12,2]{0,1:T(2,128)S(1)} copy-done((s32[12,2]{0,1:T(2,128)S(1)}, s32[12,2]{0,1:T(2,128)}, u32[]{:S(2)}) %copy-start.4) | copy-done | bytes 120
  2.0 0.7 %copy.17.tw = s32[12,2]{1,0:T(8,128)} copy(s32[12,2]{0,1:T(2,128)S(1)} %copy-done.4) | data formatting | bytes 192 | tf_op args[2]
  2.6 13.3 %halo.1 = (bf16[368,256]{1,0:T(8,128)(2,1)}, bf16[368,256]{1,0:T(8,128)(2,1)}) custom-call(bf16[736,256]{1,0:T(8,128)(2,1)} %bitcast.2), custom_call_target="tpu_custom_call" | custom-call | tf_op jit(solution)/shard_map/halo/pallas_call | solution.py:270
  15.9 9.2 %attend.1 = (bf16[12,128,256]{2,1,0:T(8,128)(2,1)}, bf16[12,128,256]{2,1,0:T(8,128)(2,1)}, f32[736,256]{1,0:T(8,128)}, bf16[736,256]{1,0:T(8,128)(2,1)}, bf16[16,64,128]{2,1,0:T(8,128)(2,1)}) custom-call(s32[12,2]{1,0:T(8,128)} %copy.17.tw, s32[1]{0:T(128)S(6)} %copy.23.cnt, bf16[12,128,256]{2,1,0:T(8,128)(2,1)} %x_ref.1, bf16[12,128,256]{2,1,0:T(8,128)(2,1)} %cot_ref.1, ...), custom_call_target="tpu_custom_call" | custom-call | tf_op jit(solution)/shard_map/attend/pallas_call | solution.py:286
  25.2 26.8 %reduce.1 = (f32[736,256]{1,0:T(8,128)}, f32[256,128]{1,0:T(8,128)}, f32[256,128]{1,0:T(8,128)}, f32[256,128]{1,0:T(8,128)}, f32[128,256]{1,0:T(8,128)}) custom-call(f32[736,256]{1,0:T(8,128)} %get-tuple-element.23.own, bf16[736,256]{1,0:T(8,128)(2,1)} %get-tuple-element.24.halo, bf16[16,64,128]{2,1,0:T(8,128)(2,1)} %get-tuple-element.25.g, ...), custom_call_target="tpu_custom_call" | custom-call | tf_op jit(solution)/shard_map/reduce/pallas_call | solution.py:317
  52.0 0.0 copy-start.3
  52.0 2.1 %copy.24 = f32[4,184,256]{2,1,0:T(8,128)} copy(f32[4,184,256]{2,1,0:T(8,128)} %bitcast.4) | data formatting | bytes 1507328
  54.1 0.0 copy-done.3
  54.1 0.0 copy-start.2
  54.1 0.7 %copy.25 = f32[256,128]{1,0:T(8,128)} copy(f32[256,128]{1,0:T(8,128)S(1)} %copy-done.3) | data formatting | bytes 262144
  54.8 0.3 copy-done.2
  55.1 0.0 copy-start.1
  55.1 0.7 %copy.26 = f32[256,128]{1,0:T(8,128)} copy(f32[256,128]{1,0:T(8,128)S(1)} %copy-done.2) | data formatting | bytes 262144
  55.7 0.3 copy-done.1
  56.0 0.0 copy-start
  56.0 0.7 %copy.27 = f32[256,128]{1,0:T(8,128)} copy(f32[256,128]{1,0:T(8,128)S(1)} %copy-done.1) | data formatting | bytes 262144
  56.7 0.3 copy-done
  57.0 0.7 %copy.28 = f32[128,256]{1,0:T(8,128)} copy(f32[128,256]{1,0:T(8,128)S(1)} %copy-done) | data formatting | bytes 262144
Async XLA Ops:
  1.3 0.7 %copy-start.4 = (s32[12,2]{0,1:T(2,128)S(1)}, s32[12,2]{0,1:T(2,128)}, u32[]{:S(2)}) copy-start(s32[12,2]{0,1:T(2,128)} %param.12) | copy-start | bytes 292
  52.0 2.1 %copy-start.3 = (f32[256,128]{1,0:T(8,128)S(1)}, f32[256,128]{1,0:T(8,128)}, u32[]{:S(2)}) copy-start(f32[256,128]{1,0:T(8,128)} %get-tuple-element.41) | copy-start | bytes 393220
  54.1 1.0 %copy-start.2 = (f32[256,128]{1,0:T(8,128)S(1)}, f32[256,128]{1,0:T(8,128)}, u32[]{:S(2)}) copy-start(f32[256,128]{1,0:T(8,128)} %get-tuple-element.42) | copy-start | bytes 393220
  55.1 1.0 %copy-start.1 = (f32[256,128]{1,0:T(8,128)S(1)}, f32[256,128]{1,0:T(8,128)}, u32[]{:S(2)}) copy-start(f32[256,128]{1,0:T(8,128)} %get-tuple-element.43) | copy-start | bytes 393220
  56.0 1.0 %copy-start = (f32[128,256]{1,0:T(8,128)S(1)}, f32[128,256]{1,0:T(8,128)}, u32[]{:S(2)}) copy-start(f32[128,256]{1,0:T(8,128)} %get-tuple-element.44) | copy-start | bytes 393220

commit v2 on v1

--- a/solution.py
+++ b/solution.py
@@ -25,25 +25,38 @@
     return lax.dot_general(a, b, dims, preferred_element_type=F32)
 
 
-def halo_kernel(n_lon, lat, low, high, send, recv):
-    me = lax.axis_index("lon")
+def send(src, dst, send_sem, recv_sem, target):
+    copy = pltpu.make_async_remote_copy(
+        src_ref=src, dst_ref=dst, send_sem=send_sem, recv_sem=recv_sem, device_id=target,
+        device_id_type=MESH)
+    copy.start()
+    return copy
+
+
+def halo_kernel(n_inst, n_lon, parts, lat, low, high, send_sem, recv_sem, fan_send, fan_recv):
+    me, mi = lax.axis_index("lon"), lax.axis_index("inst")
     right, left = lax.rem(me + 1, n_lon), lax.rem(me + n_lon - 1, n_lon)
+    peers = [lax.rem(mi + d, n_inst) for d in range(1, n_inst)] if parts > 1 else []
     barrier = pltpu.get_barrier_semaphore()
     for other in (left, right):
         pl.semaphore_signal(barrier, inc=1, device_id={"lon": other}, device_id_type=MESH)
-    pl.semaphore_wait(barrier, 2)
-    edge = low.shape[0]
-    rows = lat.shape[0]
-    up = pltpu.make_async_remote_copy(
-        src_ref=lat.at[pl.ds(rows - edge, edge)], dst_ref=low, send_sem=send.at[0],
-        recv_sem=recv.at[0], device_id={"lon": right}, device_id_type=MESH)
-    down = pltpu.make_async_remote_copy(
-        src_ref=lat.at[pl.ds(0, edge)], dst_ref=high, send_sem=send.at[1],
-        recv_sem=recv.at[1], device_id={"lon": left}, device_id_type=MESH)
-    up.start()
-    down.start()
-    up.wait()
-    down.wait()
+    for other in peers:
+        pl.semaphore_signal(barrier, inc=1, device_id={"inst": other}, device_id_type=MESH)
+    pl.semaphore_wait(barrier, 2 + len(peers))
+    mine = mi if parts > 1 else 0
+    first = send(lat.at[parts + mine], low.at[mine], send_sem.at[0], recv_sem.at[0], {"lon": right})
+    second = send(lat.at[mine], high.at[mine], send_sem.at[1], recv_sem.at[1], {"lon": left})
+    fans = []
+    for side, (copy, block) in enumerate(((first, low), (second, high))):
+        copy.wait_recv()
+        for d, other in enumerate(peers):
+            fans.append(send(
+                block.at[mine], block.at[mine], fan_send.at[side, d], fan_recv.at[side, d],
+                {"inst": other}))
+    first.wait_send()
+    second.wait_send()
+    for copy in fans:
+        copy.wait()
 
 
 def attend_kernel(
@@ -102,8 +115,8 @@
     att_parts, query_parts = [], []
     for j in range(tiles):
         t = step * tiles + j
-        col = lax.rem(tw[t, 0] - band_first + REACH + lon_cols, lon_cols)
-        base = col * lat_rows + tw[t, 1]
+        col = lax.rem(tw[0, t] - band_first + REACH + lon_cols, lon_cols)
+        base = col * lat_rows + tw[1, t]
         q_t = queries[j * length : (j + 1) * length]
         g_t = att_grad[j * length : (j + 1) * length]
         spans = [pl.ds(base + a * lat_rows, SUB) for a in range(WINDOW)]
@@ -138,10 +151,13 @@
 
     @pl.when(step == pl.num_programs(0) - 1)
     def _():
+        half = own_out.shape[1]
+        parts = own_out.shape[0] // 2
         for ref, lanes in ((kg, pl.ds(0, attn)), (vg, pl.ds(attn, attn))):
-            own_out[:, lanes] = ref[pl.ds(edge, own_rows), :]
-            halo_out[pl.ds(0, edge), lanes] = ref[pl.ds(0, edge), :].astype(BF16)
-            halo_out[pl.ds(edge, edge), lanes] = ref[pl.ds(edge + own_rows, edge), :].astype(BF16)
+            for k in range(2 * parts):
+                own_out[k, :, lanes] = ref[pl.ds(edge + k * half, half), :]
+                at = k * half if k < parts else own_rows + k * half
+                halo_out[k, :, lanes] = ref[pl.ds(at, half), :].astype(BF16)
         kv = jnp.zeros((width, 2 * attn), F32)
         for ref, first, count in ((low, 0, edge), (lat, edge, own_rows), (high, edge + own_rows, edge)):
             rows_at = pl.ds(first, count)
@@ -159,13 +175,12 @@
 
 
 def reduce_kernel(
-    n_inst, n_lon, own, halo, g, wk, wv, lat_out, q_out, k_out, v_out, o_out,
-    hbuf, shares, rs, part, ag, h_s, h_r, i_s, i_r, rs_s, rs_r, p_s, p_r, a_s, a_r,
+    n_inst, n_lon, parts, own, halo, g, shares, ag,
+    pre, hsum, hbuf, share, rs, part, mine, b_s, b_r, h_s, h_r, i_s, i_r, rs_s, rs_r,
+    p_s, p_r, a_s, a_r, local,
 ):
     me, mi = lax.axis_index("lon"), lax.axis_index("inst")
-    edge = hbuf.shape[1]
-    own_rows = own.shape[0]
-    attn = wk.shape[1]
+    slot = mi if parts > 1 else 0
 
     def lon_at(d):
         return lax.rem(me + d, n_lon)
@@ -180,21 +195,30 @@
         pl.semaphore_signal(barrier, inc=1, device_id={"inst": inst_at(d)}, device_id_type=MESH)
     pl.semaphore_wait(barrier, n_lon + n_inst - 2)
 
-    def send(src, dst, s, r, target):
-        copy = pltpu.make_async_remote_copy(
-            src_ref=src, dst_ref=dst, send_sem=s, recv_sem=r, device_id=target,
-            device_id_type=MESH)
-        copy.start()
-        return copy
-
-    halos = [
-        send(halo.at[pl.ds(0, edge)], hbuf.at[0], h_s.at[0], h_r.at[0], {"lon": lon_at(n_lon - 1)}),
-        send(halo.at[pl.ds(edge, edge)], hbuf.at[1], h_s.at[1], h_r.at[1], {"lon": lon_at(1)}),
-    ]
+    joined = []
+    if parts > 1:
+        for side in range(2):
+            for d in range(1, n_inst):
+                joined.append(send(
+                    halo.at[side * parts + inst_at(d)], pre.at[side, d], b_s.at[side, d],
+                    b_r.at[side, d], {"inst": inst_at(d)}))
     scatters = [
         send(g.at[lon_at(d)], rs.at[d], rs_s.at[d], rs_r.at[d], {"lon": lon_at(d)})
         for d in range(1, n_lon)
     ]
+    for k in range(2 * parts):
+        share[k] = own[k].astype(BF16)
+    for copy in joined:
+        copy.wait()
+    halos = []
+    for side, d in ((0, n_lon - 1), (1, 1)):
+        total = halo[side * parts + slot].astype(F32)
+        if parts > 1:
+            for e in range(1, n_inst):
+                total = total + pre[side, e].astype(F32)
+        hsum[side] = total.astype(BF16)
+        halos.append(send(
+            hsum.at[side], hbuf.at[side], h_s.at[side], h_r.at[side], {"lon": lon_at(d)}))
     for copy in scatters:
         copy.wait()
     total = g[me].astype(F32)
@@ -205,51 +229,53 @@
         send(part.at[mi], part.at[mi], p_s.at[d], p_r.at[d], {"inst": inst_at(d)})
         for d in range(1, n_inst)
     ]
-    for copy in halos:
-        copy.wait()
-    shares[mi, pl.ds(0, edge), :] = (own[pl.ds(0, edge), :] + hbuf[1].astype(F32)).astype(BF16)
-    shares[mi, pl.ds(own_rows - edge, edge), :] = (
-        own[pl.ds(own_rows - edge, edge), :] + hbuf[0].astype(F32)
-    ).astype(BF16)
-    joins = [
-        send(shares.at[mi], shares.at[mi], i_s.at[d], i_r.at[d], {"inst": inst_at(d)})
-        for d in range(1, n_inst)
-    ]
     for copy in swaps:
         copy.wait()
     total = part[0]
     for i in range(1, n_inst):
         total = total + part[i]
-    ag[me] = total.astype(BF16)
+    mine[...] = total.astype(BF16)
     gathers = [
-        send(ag.at[me], ag.at[me], a_s.at[d], a_r.at[d], {"lon": lon_at(d)})
+        send(mine, ag.at[me], a_s.at[d], a_r.at[d], {"lon": lon_at(d)})
         for d in range(1, n_lon)
     ]
+    gathers.append(pltpu.make_async_copy(mine, ag.at[me], local.at[0]))
+    gathers[-1].start()
+    for copy in halos:
+        copy.wait()
+    share[slot] = (own[slot] + hbuf[1].astype(F32)).astype(BF16)
+    share[parts + slot] = (own[parts + slot] + hbuf[0].astype(F32)).astype(BF16)
+    joins = [
+        send(share, shares.at[mi], i_s.at[d], i_r.at[d], {"inst": inst_at(d)})
+        for d in range(1, n_inst)
+    ]
+    joins.append(pltpu.make_async_copy(share, shares.at[mi], local.at[1]))
+    joins[-1].start()
     for copy in joins:
         copy.wait()
-    grad = shares[0].astype(F32)
-    for i in range(1, n_inst):
-        grad = grad + shares[i].astype(F32)
+    for copy in gathers:
+        copy.wait()
+
+
+def finish_kernel(shares, ag, wk, wv, lat_out, q_out, k_out, v_out, o_out):
+    attn = wk.shape[1]
+    grad = shares[0, 0].astype(F32)
+    for i in range(1, shares.shape[0]):
+        grad = grad + shares[i, 0].astype(F32)
     grad_high = grad.astype(BF16)
     grad_low = (grad - grad_high.astype(F32)).astype(BF16)
     w_pair = jnp.concatenate([wk[...], wv[...]], axis=1)
     lat_out[...] = dot(grad_high, w_pair, NT) + dot(grad_low, w_pair, NT)
-    for copy in gathers:
-        copy.wait()
-    rows = ag.shape[1]
-    at = 0
-
-    def take(count):
-        nonlocal at
-        block = ag[pl.ds(at, count // rows)].astype(F32).reshape(count, attn)
-        at += count // rows
-        return block
-
-    q_out[...] = take(q_out.shape[0])
-    k_out[...] = take(k_out.shape[0])
-    v_out[...] = take(v_out.shape[0])
-    o_out[:, pl.ds(0, attn)] = take(o_out.shape[0])
-    o_out[:, pl.ds(attn, attn)] = take(o_out.shape[0])
+
+    @pl.when(pl.program_id(0) == 0)
+    def _():
+        rows = ag.shape[1]
+        at = 0
+        out_parts = [o_out.at[:, pl.ds(0, attn)], o_out.at[:, pl.ds(attn, attn)]]
+        for out in [q_out, k_out, v_out] + out_parts:
+            count = out.shape[0] // rows
+            out[...] = ag[pl.ds(at, count)].astype(F32).reshape(out.shape)
+            at += count
 
 
 def vmem():
@@ -266,16 +292,20 @@
     edge, own_rows = REACH * lat_rows, band_cols * lat_rows
     wide = own_rows + 2 * edge
     flat = latents.reshape(own_rows, width)
+    parts = n_inst if edge % (SUB * n_inst) == 0 else 1
+    half = edge // parts
     dma = pltpu.SemaphoreType.DMA
+    anywhere = pl.BlockSpec(memory_space=pl.ANY)
     low, high = pl.pallas_call(
-        functools.partial(halo_kernel, n_lon),
-        out_shape=[jax.ShapeDtypeStruct((edge, width), BF16)] * 2,
-        in_specs=[pl.BlockSpec(memory_space=pl.ANY)],
-        out_specs=[pl.BlockSpec(memory_space=pl.ANY)] * 2,
-        scratch_shapes=[dma((2,)), dma((2,))],
+        functools.partial(halo_kernel, n_inst, n_lon, parts),
+        out_shape=[jax.ShapeDtypeStruct((parts, half, width), BF16)] * 2,
+        in_specs=[anywhere],
+        out_specs=[anywhere] * 2,
+        scratch_shapes=[dma((2,)), dma((2,)), dma((2, n_inst)), dma((2, n_inst))],
         compiler_params=pltpu.CompilerParams(collective_id=0, has_side_effects=True),
         name="halo",
-    )(flat)
+    )(latents.reshape(2 * parts, half, width))
+    low, high = low.reshape(edge, width), high.reshape(edge, width)
 
     group = next(b for b in (4, 3, 2, 1) if n_tiles % b == 0)
     weight_rows = 2 * width + 2 * attn + width
@@ -289,8 +319,8 @@
         out_shape=[
             jax.ShapeDtypeStruct(obs_x.shape, BF16),
             jax.ShapeDtypeStruct(obs_x.shape, BF16),
-            jax.ShapeDtypeStruct((own_rows, 2 * attn), F32),
-            jax.ShapeDtypeStruct((2 * edge, 2 * attn), BF16),
+            jax.ShapeDtypeStruct((2 * parts, half, 2 * attn), F32),
+            jax.ShapeDtypeStruct((2 * parts, half, 2 * attn), BF16),
             jax.ShapeDtypeStruct((n_lon, rows, attn), BF16),
         ],
         in_specs=[
@@ -299,7 +329,7 @@
             whole(width, attn), whole(attn, width),
         ],
         out_specs=[
-            tile_spec, tile_spec, whole(own_rows, 2 * attn), whole(2 * edge, 2 * attn),
+            tile_spec, tile_spec, whole(2 * parts, half, 2 * attn), whole(2 * parts, half, 2 * attn),
             whole(n_lon, rows, attn),
         ],
         scratch_shapes=[
@@ -311,11 +341,39 @@
             pltpu.VMEM((attn, width), F32),
         ],
         name="attend",
-    )(tile_window, band_counts, obs_x, obs_cot, point_mask, flat, low, high,
+    )(tile_window.T, band_counts, obs_x, obs_cot, point_mask, flat, low, high,
       w_query, w_key, w_value, w_out)
 
+    shares, ag = pl.pallas_call(
+        functools.partial(reduce_kernel, n_inst, n_lon, parts),
+        out_shape=[
+            jax.ShapeDtypeStruct((n_inst, 2 * parts, half, 2 * attn), BF16),
+            jax.ShapeDtypeStruct((n_lon, rows, attn), BF16),
+        ],
+        in_specs=[vmem()] * 3,
+        out_specs=[anywhere] * 2,
+        scratch_shapes=[
+            pltpu.VMEM((2, n_inst, half, 2 * attn), BF16),
+            pltpu.VMEM((2, half, 2 * attn), BF16),
+            pltpu.VMEM((2, half, 2 * attn), BF16),
+            pltpu.VMEM((2 * parts, half, 2 * attn), BF16),
+            pltpu.VMEM((n_lon, rows, attn), BF16),
+            pltpu.VMEM((n_inst, rows, attn), F32),
+            pltpu.VMEM((rows, attn), BF16),
+            dma((2, n_inst)), dma((2, n_inst)),
+            dma((2,)), dma((2,)),
+            dma((n_inst,)), dma((n_inst,)),
+            dma((n_lon,)), dma((n_lon,)),
+            dma((n_inst,)), dma((n_inst,)),
+            dma((n_lon,)), dma((n_lon,)),
+            dma((2,)),
+        ],
+        compiler_params=pltpu.CompilerParams(collective_id=1, has_side_effects=True),
+        name="reduce",
+    )(own, halo, g)
     latent_grad, query_grad, key_grad, value_grad, out_grad = pl.pallas_call(
-        functools.partial(reduce_kernel, n_inst, n_lon),
+        finish_kernel,
+        grid=(2 * parts,),
         out_shape=[
             jax.ShapeDtypeStruct((own_rows, width), F32),
             jax.ShapeDtypeStruct((width, attn), F32),
@@ -323,23 +381,16 @@
             jax.ShapeDtypeStruct((width, attn), F32),
             jax.ShapeDtypeStruct((attn, width), F32),
         ],
-        in_specs=[vmem()] * 5,
-        out_specs=[vmem()] * 5,
-        scratch_shapes=[
-            pltpu.VMEM((2, edge, 2 * attn), BF16),
-            pltpu.VMEM((n_inst, own_rows, 2 * attn), BF16),
-            pltpu.VMEM((n_lon, rows, attn), BF16),
-            pltpu.VMEM((n_inst, rows, attn), F32),
-            pltpu.VMEM((n_lon, rows, attn), BF16),
-            dma((2,)), dma((2,)),
-            dma((n_inst,)), dma((n_inst,)),
-            dma((n_lon,)), dma((n_lon,)),
-            dma((n_inst,)), dma((n_inst,)),
-            dma((n_lon,)), dma((n_lon,)),
-        ],
-        compiler_params=pltpu.CompilerParams(collective_id=1, has_side_effects=True),
-        name="reduce",
-    )(own, halo, g, w_key, w_value)
+        in_specs=[
+            pl.BlockSpec((n_inst, 1, half, 2 * attn), lambda i: (0, i, 0, 0)),
+            whole(n_lon, rows, attn), whole(width, attn), whole(width, attn),
+        ],
+        out_specs=[
+            pl.BlockSpec((half, width), lambda i: (i, 0)), whole(width, attn),
+            whole(width, attn), whole(width, attn), whole(attn, width),
+        ],
+        name="finish",
+    )(shares, ag, w_key, w_value)
     return (
         decoded,
         obs_grad,

time: 57.9 us -> 50.4 us (0.87)
  local copies, waits for them, and re-layouts: 6.94 us -> 0 us
  Pallas kernels: 49.4 us -> 48.8 us
    unnamed x16 -> x0, local copies, waits for them, and re-layouts: 6.94 us -> none
    pallas_call x2 -> x3, Pallas kernels: 40.1 us -> 39.6 us  [the longest x1 23.3 us: shards(): pl.pallas_call(functools.partial(reduce_kernel, n_inst, n_lon, parts), ou...]
where the time goes in v2:
time: 50.4 us; the launch traced here: 50.1 us
  Pallas kernels  48.8 us (97%)
  between operations  1.3 us (3%)
    pallas_call x1, Pallas kernels, shards(): pl.pallas_call(functools.partial(reduce_kernel, n_inst, n_lon, parts), ou...  23.3 us
    pallas_call x1, Pallas kernels, shards(): pl.pallas_call(functools.partial(halo_kernel, n_inst, n_lon, parts), out_...  12.2 us
    pallas_call x1, Pallas kernels, shards(): pl.pallas_call(functools.partial(attend_kernel, band_cols * n_lon, lat_ro...  9.21 us
    pallas_call x1, Pallas kernels, shards(): pl.pallas_call(finish_kernel, grid=(2 * parts,), out_shape=[jax.ShapeDtyp...  4.13 us

profile of v2, /device:TPU:0, one launch (start us, length us, event | category | flops | bytes accessed | tf_op | source)
XLA Modules:
  0.0 50.1 jit_solution(1384712891301121402)
XLA Ops:
  1.3 12.2 %halo.1 = (bf16[2,184,256]{2,1,0:T(8,128)(2,1)}, bf16[2,184,256]{2,1,0:T(8,128)(2,1)}) custom-call(bf16[4,184,256]{2,1,0:T(8,128)(2,1)} %lat.1), custom_call_target="tpu_custom_call" | custom-call | tf_op jit(solution)/shard_map/halo/pallas_call | solution.py:299
  13.5 9.2 %attend.1 = (bf16[12,128,256]{2,1,0:T(8,128)(2,1)}, bf16[12,128,256]{2,1,0:T(8,128)(2,1)}, f32[4,184,256]{2,1,0:T(8,128)}, bf16[4,184,256]{2,1,0:T(8,128)(2,1)}, bf16[16,64,128]{2,1,0:T(8,128)(2,1)}) custom-call(s32[2,12]{1,0:T(2,128)} %bitcast.8, s32[1]{0:T(128)S(6)} %copy.17.cnt, bf16[12,128,256]{2,1,0:T(8,128)(2,1)} %x_ref.1, ...), custom_call_target="tpu_custom_call" | custom-call | tf_op jit(solution)/shard_map/attend/pallas_call | solution.py:316
  22.7 23.3 %reduce.1 = (bf16[2,4,184,256]{3,2,1,0:T(8,128)(2,1)}, bf16[16,64,128]{2,1,0:T(8,128)(2,1)}) custom-call(f32[4,184,256]{2,1,0:T(8,128)} %get-tuple-element.25.own, bf16[4,184,256]{2,1,0:T(8,128)(2,1)} %get-tuple-element.26.halo, bf16[16,64,128]{2,1,0:T(8,128)(2,1)} %get-tuple-element.27.g), custom_call_target="tpu_custom_call" | custom-call | tf_op jit(solution)/shard_map/reduce/pallas_call | solution.py:347
  46.0 4.1 %finish.1 = (f32[736,256]{1,0:T(8,128)}, f32[256,128]{1,0:T(8,128)}, f32[256,128]{1,0:T(8,128)}, f32[256,128]{1,0:T(8,128)}, f32[128,256]{1,0:T(8,128)}) custom-call(bf16[2,4,184,256]{3,2,1,0:T(8,128)(2,1)} %get-tuple-element.28.shares, bf16[16,64,128]{2,1,0:T(8,128)(2,1)} %get-tuple-element.29.ag, bf16[256,128]{1,0:T(8,128)(2,1)} %wk.3, bf16[256,128]{1,0:T(8,128)(2,1)} %wv.3), custom_call_target="tpu_custom_call" | custom-call | tf_op jit(solution)/shard_map/finish/pallas_call | solution.py:374

commit v3 on v2

--- a/solution.py
+++ b/solution.py
@@ -33,7 +33,27 @@
     return copy
 
 
-def halo_kernel(n_inst, n_lon, parts, lat, low, high, send_sem, recv_sem, fan_send, fan_recv):
+def live_rows(mask_ref, cnt, first, tiles, width):
+    length = mask_ref.shape[1]
+    row_id = lax.broadcasted_iota(jnp.int32, (length, width), 0)
+    blocks = []
+    for j in range(tiles):
+        t = first + j
+        used = jnp.sum(mask_ref[pl.ds(t, 1), :], axis=1, keepdims=True)
+        used = jnp.where(t < cnt[0], used, 0)
+        blocks.append((row_id < used).astype(F32))
+    return jnp.concatenate(blocks, axis=0)
+
+
+def halo_kernel(
+    n_inst, n_lon, parts, group, lat, x_hbm, cot_hbm, mask_ref, cnt, wq, wo,
+    low, high, q_hbm, g_hbm, x_ref, cot_ref, q_ref, g_ref,
+    send_sem, recv_sem, fan_send, fan_recv, load, store,
+):
+    loads = [pltpu.make_async_copy(x_hbm, x_ref, load.at[0]),
+             pltpu.make_async_copy(cot_hbm, cot_ref, load.at[1])]
+    for copy in loads:
+        copy.start()
     me, mi = lax.axis_index("lon"), lax.axis_index("inst")
     right, left = lax.rem(me + 1, n_lon), lax.rem(me + n_lon - 1, n_lon)
     peers = [lax.rem(mi + d, n_inst) for d in range(1, n_inst)] if parts > 1 else []
@@ -46,6 +66,21 @@
     mine = mi if parts > 1 else 0
     first = send(lat.at[parts + mine], low.at[mine], send_sem.at[0], recv_sem.at[0], {"lon": right})
     second = send(lat.at[mine], high.at[mine], send_sem.at[1], recv_sem.at[1], {"lon": left})
+    for copy in loads:
+        copy.wait()
+    n_tiles, length, width = x_ref.shape
+    for k in range(0, n_tiles, group):
+        at = pl.ds(k, group)
+        shape = (group, length, q_ref.shape[2])
+        flat = x_ref[at].reshape(group * length, width)
+        q_ref[at] = dot(flat, wq[...]).astype(BF16).reshape(shape)
+        live = live_rows(mask_ref, cnt, k, group, width)
+        masked = (cot_ref[at].reshape(group * length, width).astype(F32) * live).astype(BF16)
+        g_ref[at] = dot(masked, wo[...], NT).astype(BF16).reshape(shape)
+    stores = [pltpu.make_async_copy(q_ref, q_hbm, store.at[0]),
+              pltpu.make_async_copy(g_ref, g_hbm, store.at[1])]
+    for copy in stores:
+        copy.start()
     fans = []
     for side, (copy, block) in enumerate(((first, low), (second, high))):
         copy.wait_recv()
@@ -55,12 +90,12 @@
                 {"inst": other}))
     first.wait_send()
     second.wait_send()
-    for copy in fans:
+    for copy in fans + stores:
         copy.wait()
 
 
 def attend_kernel(
-    lon_cols, lat_rows, tw, cnt, x_ref, cot_ref, mask_ref, lat, low, high, wq, wk, wv, wo,
+    lon_cols, lat_rows, tw, cnt, x_ref, cot_ref, q_ref, g_ref, mask_ref, lat, low, high, wq, wk, wv, wo,
     dec, og, own_out, halo_out, g_out, keys, values, kg, vg, qg, outg,
 ):
     step = pl.program_id(0)
@@ -93,18 +128,8 @@
 
     flat_x = x_ref[...].reshape(tiles * length, width)
     flat_cot = cot_ref[...].reshape(tiles * length, width)
-    queries = dot(flat_x, wq[...]).astype(BF16)
-
-    row_id = lax.broadcasted_iota(jnp.int32, (length, width), 0)
-    lives = []
-    for j in range(tiles):
-        t = step * tiles + j
-        used = jnp.sum(mask_ref[pl.ds(t, 1), :], axis=1, keepdims=True)
-        used = jnp.where(t < cnt[0], used, 0)
-        lives.append(row_id < used)
-    live = jnp.concatenate([m.astype(F32) for m in lives], axis=0)
+    live = live_rows(mask_ref, cnt, step * tiles, tiles, width)
     masked = (flat_cot.astype(F32) * live).astype(BF16)
-    att_grad = dot(masked, wo[...], NT).astype(BF16)
 
     lane = lax.broadcasted_iota(jnp.int32, (1, attn), 1) // head
     head_mask = [(lane == h).astype(F32) for h in range(HEADS)]
@@ -117,8 +142,8 @@
         t = step * tiles + j
         col = lax.rem(tw[0, t] - band_first + REACH + lon_cols, lon_cols)
         base = col * lat_rows + tw[1, t]
-        q_t = queries[j * length : (j + 1) * length]
-        g_t = att_grad[j * length : (j + 1) * length]
+        q_t = q_ref[j]
+        g_t = g_ref[j]
         spans = [pl.ds(base + a * lat_rows, SUB) for a in range(WINDOW)]
         kw = jnp.concatenate([keys[at, :] for at in spans], axis=0)
         vw = jnp.concatenate([values[at, :] for at in spans], axis=0)
@@ -175,9 +200,9 @@
 
 
 def reduce_kernel(
-    n_inst, n_lon, parts, own, halo, g, shares, ag,
-    pre, hsum, hbuf, share, rs, part, mine, b_s, b_r, h_s, h_r, i_s, i_r, rs_s, rs_r,
-    p_s, p_r, a_s, a_r, local,
+    n_inst, n_lon, parts, gp, own, halo, g, shares, ag,
+    pre, hsum, hbuf, share, rs, part, mine, gpre, gsum, b_s, b_r, h_s, h_r, i_s, i_r, rs_s, rs_r,
+    p_s, p_r, a_s, a_r, f_s, f_r, local,
 ):
     me, mi = lax.axis_index("lon"), lax.axis_index("inst")
     slot = mi if parts > 1 else 0
@@ -195,19 +220,33 @@
         pl.semaphore_signal(barrier, inc=1, device_id={"inst": inst_at(d)}, device_id_type=MESH)
     pl.semaphore_wait(barrier, n_lon + n_inst - 2)
 
-    joined = []
+    joined, presums = [], []
+    if gp > 1:
+        presums = [
+            send(g.at[pl.ds(inst_at(d) * n_lon, n_lon)], gpre.at[d], p_s.at[d], p_r.at[d],
+                 {"inst": inst_at(d)})
+            for d in range(1, n_inst)
+        ]
     if parts > 1:
         for side in range(2):
             for d in range(1, n_inst):
                 joined.append(send(
                     halo.at[side * parts + inst_at(d)], pre.at[side, d], b_s.at[side, d],
                     b_r.at[side, d], {"inst": inst_at(d)}))
+    if gp > 1:
+        for copy in presums:
+            copy.wait()
+        total = g[pl.ds(mi * n_lon, n_lon)].astype(F32)
+        for d in range(1, n_inst):
+            total = total + gpre[d].astype(F32)
+        gsum[...] = total.astype(BF16)
+        source = gsum
+    else:
+        source = g
     scatters = [
-        send(g.at[lon_at(d)], rs.at[d], rs_s.at[d], rs_r.at[d], {"lon": lon_at(d)})
+        send(source.at[lon_at(d)], rs.at[d], rs_s.at[d], rs_r.at[d], {"lon": lon_at(d)})
         for d in range(1, n_lon)
     ]
-    for k in range(2 * parts):
-        share[k] = own[k].astype(BF16)
     for copy in joined:
         copy.wait()
     halos = []
@@ -219,28 +258,38 @@
         hsum[side] = total.astype(BF16)
         halos.append(send(
             hsum.at[side], hbuf.at[side], h_s.at[side], h_r.at[side], {"lon": lon_at(d)}))
+    for k in range(2 * parts):
+        share[k] = own[k].astype(BF16)
     for copy in scatters:
         copy.wait()
-    total = g[me].astype(F32)
+    total = source[me].astype(F32)
     for d in range(1, n_lon):
         total = total + rs[d].astype(F32)
-    part[mi] = total
-    swaps = [
-        send(part.at[mi], part.at[mi], p_s.at[d], p_r.at[d], {"inst": inst_at(d)})
-        for d in range(1, n_inst)
-    ]
-    for copy in swaps:
-        copy.wait()
-    total = part[0]
-    for i in range(1, n_inst):
-        total = total + part[i]
+    if gp == 1:
+        part[mi] = total
+        swaps = [
+            send(part.at[mi], part.at[mi], p_s.at[d], p_r.at[d], {"inst": inst_at(d)})
+            for d in range(1, n_inst)
+        ]
+        for copy in swaps:
+            copy.wait()
+        total = part[0]
+        for i in range(1, n_inst):
+            total = total + part[i]
     mine[...] = total.astype(BF16)
+    base = mi * n_lon if gp > 1 else 0
     gathers = [
-        send(mine, ag.at[me], a_s.at[d], a_r.at[d], {"lon": lon_at(d)})
+        send(mine, ag.at[base + me], a_s.at[d], a_r.at[d], {"lon": lon_at(d)})
         for d in range(1, n_lon)
     ]
-    gathers.append(pltpu.make_async_copy(mine, ag.at[me], local.at[0]))
-    gathers[-1].start()
+    fans = []
+    if gp > 1:
+        fans = [
+            send(mine, ag.at[base + me], f_s.at[d, 0], f_r.at[d, 0], {"inst": inst_at(d)})
+            for d in range(1, n_inst)
+        ]
+    keep = pltpu.make_async_copy(mine, ag.at[base + me], local.at[0])
+    keep.start()
     for copy in halos:
         copy.wait()
     share[slot] = (own[slot] + hbuf[1].astype(F32)).astype(BF16)
@@ -251,9 +300,16 @@
     ]
     joins.append(pltpu.make_async_copy(share, shares.at[mi], local.at[1]))
     joins[-1].start()
-    for copy in joins:
-        copy.wait()
+    for e, copy in enumerate(gathers, 1):
+        copy.wait_recv()
+        if gp > 1:
+            at = base + lon_at(n_lon - e)
+            for d in range(1, n_inst):
+                fans.append(send(
+                    ag.at[at], ag.at[at], f_s.at[d, e], f_r.at[d, e], {"inst": inst_at(d)}))
     for copy in gathers:
+        copy.wait_send()
+    for copy in joins + fans + [keep]:
         copy.wait()
 
 
@@ -296,23 +352,32 @@
     half = edge // parts
     dma = pltpu.SemaphoreType.DMA
     anywhere = pl.BlockSpec(memory_space=pl.ANY)
-    low, high = pl.pallas_call(
-        functools.partial(halo_kernel, n_inst, n_lon, parts),
-        out_shape=[jax.ShapeDtypeStruct((parts, half, width), BF16)] * 2,
-        in_specs=[anywhere],
-        out_specs=[anywhere] * 2,
-        scratch_shapes=[dma((2,)), dma((2,)), dma((2, n_inst)), dma((2, n_inst))],
+    group = next(b for b in (4, 3, 2, 1) if n_tiles % b == 0)
+    smem = pl.BlockSpec(memory_space=pltpu.SMEM)
+    low, high, queries, att_grad = pl.pallas_call(
+        functools.partial(halo_kernel, n_inst, n_lon, parts, group),
+        out_shape=[jax.ShapeDtypeStruct((parts, half, width), BF16)] * 2
+        + [jax.ShapeDtypeStruct((n_tiles, length, attn), BF16)] * 2,
+        in_specs=[anywhere] * 3 + [vmem(), smem, vmem(), vmem()],
+        out_specs=[anywhere] * 4,
+        scratch_shapes=[
+            pltpu.VMEM(obs_x.shape, BF16), pltpu.VMEM(obs_x.shape, BF16),
+            pltpu.VMEM((n_tiles, length, attn), BF16), pltpu.VMEM((n_tiles, length, attn), BF16),
+            dma((2,)), dma((2,)), dma((2, n_inst)), dma((2, n_inst)), dma((2,)), dma((2,)),
+        ],
         compiler_params=pltpu.CompilerParams(collective_id=0, has_side_effects=True),
         name="halo",
-    )(latents.reshape(2 * parts, half, width))
+    )(latents.reshape(2 * parts, half, width), obs_x, obs_cot, point_mask, band_counts,
+      w_query, w_out)
     low, high = low.reshape(edge, width), high.reshape(edge, width)
 
-    group = next(b for b in (4, 3, 2, 1) if n_tiles % b == 0)
     weight_rows = 2 * width + 2 * attn + width
     rows = weight_rows // n_lon
+    gp = n_inst if rows % (2 * SUB * n_inst) == 0 else 1
+    rows = rows // gp
+    head_spec = pl.BlockSpec((group, length, attn), lambda i: (i, 0, 0))
     whole = lambda *shape: pl.BlockSpec(shape, lambda i: (0,) * len(shape))
     tile_spec = pl.BlockSpec((group, length, width), lambda i: (i, 0, 0))
-    smem = pl.BlockSpec(memory_space=pltpu.SMEM)
     decoded, obs_grad, own, halo, g = pl.pallas_call(
         functools.partial(attend_kernel, band_cols * n_lon, lat_rows),
         grid=(n_tiles // group,),
@@ -321,16 +386,16 @@
             jax.ShapeDtypeStruct(obs_x.shape, BF16),
             jax.ShapeDtypeStruct((2 * parts, half, 2 * attn), F32),
             jax.ShapeDtypeStruct((2 * parts, half, 2 * attn), BF16),
-            jax.ShapeDtypeStruct((n_lon, rows, attn), BF16),
+            jax.ShapeDtypeStruct((gp * n_lon, rows, attn), BF16),
         ],
         in_specs=[
-            smem, smem, tile_spec, tile_spec, whole(n_tiles, length), whole(own_rows, width),
+            smem, smem, tile_spec, tile_spec, head_spec, head_spec, whole(n_tiles, length), whole(own_rows, width),
             whole(edge, width), whole(edge, width), whole(width, attn), whole(width, attn),
             whole(width, attn), whole(attn, width),
         ],
         out_specs=[
             tile_spec, tile_spec, whole(2 * parts, half, 2 * attn), whole(2 * parts, half, 2 * attn),
-            whole(n_lon, rows, attn),
+            whole(gp * n_lon, rows, attn),
         ],
         scratch_shapes=[
             pltpu.VMEM((wide + SUB, attn), F32),
@@ -341,14 +406,14 @@
             pltpu.VMEM((attn, width), F32),
         ],
         name="attend",
-    )(tile_window.T, band_counts, obs_x, obs_cot, point_mask, flat, low, high,
+    )(tile_window.T, band_counts, obs_x, obs_cot, queries, att_grad, point_mask, flat, low, high,
       w_query, w_key, w_value, w_out)
 
     shares, ag = pl.pallas_call(
-        functools.partial(reduce_kernel, n_inst, n_lon, parts),
+        functools.partial(reduce_kernel, n_inst, n_lon, parts, gp),
         out_shape=[
             jax.ShapeDtypeStruct((n_inst, 2 * parts, half, 2 * attn), BF16),
-            jax.ShapeDtypeStruct((n_lon, rows, attn), BF16),
+            jax.ShapeDtypeStruct((gp * n_lon, rows, attn), BF16),
         ],
         in_specs=[vmem()] * 3,
         out_specs=[anywhere] * 2,
@@ -360,12 +425,15 @@
             pltpu.VMEM((n_lon, rows, attn), BF16),
             pltpu.VMEM((n_inst, rows, attn), F32),
             pltpu.VMEM((rows, attn), BF16),
+            pltpu.VMEM((n_inst, n_lon, rows, attn), BF16),
+            pltpu.VMEM((n_lon, rows, attn), BF16),
             dma((2, n_inst)), dma((2, n_inst)),
             dma((2,)), dma((2,)),
             dma((n_inst,)), dma((n_inst,)),
             dma((n_lon,)), dma((n_lon,)),
             dma((n_inst,)), dma((n_inst,)),
             dma((n_lon,)), dma((n_lon,)),
+            dma((n_inst, n_lon)), dma((n_inst, n_lon)),
             dma((2,)),
         ],
         compiler_params=pltpu.CompilerParams(collective_id=1, has_side_effects=True),
@@ -383,7 +451,7 @@
         ],
         in_specs=[
             pl.BlockSpec((n_inst, 1, half, 2 * attn), lambda i: (0, i, 0, 0)),
-            whole(n_lon, rows, attn), whole(width, attn), whole(width, attn),
+            whole(gp * n_lon, rows, attn), whole(width, attn), whole(width, attn),
         ],
         out_specs=[
             pl.BlockSpec((half, width), lambda i: (i, 0)), whole(width, attn),

time: 50.4 us -> 48.7 us (0.966)
  Pallas kernels: 48.8 us -> 47.1 us
    pallas_call x2, Pallas kernels: 35.5 us -> 33.9 us  [the longest x1 20.8 us: shards(): pl.pallas_call(functools.partial(reduce_kernel, n_inst, n_lon, parts, gp)...]
where the time goes in v3:
time: 48.7 us; the launch traced here: 48.4 us
  Pallas kernels  47.1 us (97%)
  between operations  1.3 us (3%)
    pallas_call x1, Pallas kernels, shards(): pl.pallas_call(functools.partial(reduce_kernel, n_inst, n_lon, parts, gp)...  20.8 us
    pallas_call x1, Pallas kernels, shards(): pl.pallas_call(functools.partial(halo_kernel, n_inst, n_lon, parts, group...  13.1 us
    pallas_call x1, Pallas kernels, shards(): pl.pallas_call(functools.partial(attend_kernel, band_cols * n_lon, lat_ro...  9.07 us
    pallas_call x1, Pallas kernels, shards(): pl.pallas_call(finish_kernel, grid=(2 * parts,), out_shape=[jax.ShapeDtyp...  4.13 us

profile of v3, /device:TPU:0, one launch (start us, length us, event | category | flops | bytes accessed | tf_op | source)
XLA Modules:
  0.0 48.4 jit_solution(7895265952153107830)
XLA Ops:
  1.3 13.1 %halo.1 = (bf16[2,184,256]{2,1,0:T(8,128)(2,1)}, bf16[2,184,256]{2,1,0:T(8,128)(2,1)}, bf16[12,128,128]{2,1,0:T(8,128)(2,1)}, bf16[12,128,128]{2,1,0:T(8,128)(2,1)}) custom-call(bf16[4,184,256]{2,1,0:T(8,128)(2,1)} %lat.1, bf16[12,128,256]{2,1,0:T(8,128)(2,1)} %x_ref.1, bf16[12,128,256]{2,1,0:T(8,128)(2,1)} %cot_ref.1, s32[12,128]{1,0:T(8,128)} %mask_ref.3, ...), custom_call_target="tpu_custom_call" | custom-call | tf_op jit(solution)/shard_map/halo/pallas_call | solution.py:357
  14.4 9.1 %attend.1 = (bf16[12,128,256]{2,1,0:T(8,128)(2,1)}, bf16[12,128,256]{2,1,0:T(8,128)(2,1)}, f32[4,184,256]{2,1,0:T(8,128)}, bf16[4,184,256]{2,1,0:T(8,128)(2,1)}, bf16[32,32,128]{2,1,0:T(8,128)(2,1)}) custom-call(s32[2,12]{1,0:T(2,128)} %bitcast.8, s32[1]{0:T(128)S(6)} %copy.17.cnt, bf16[12,128,256]{2,1,0:T(8,128)(2,1)} %x_ref.1, ...), custom_call_target="tpu_custom_call" | custom-call | tf_op jit(solution)/shard_map/attend/pallas_call | solution.py:381
  23.5 20.8 %reduce.1 = (bf16[2,4,184,256]{3,2,1,0:T(8,128)(2,1)}, bf16[32,32,128]{2,1,0:T(8,128)(2,1)}) custom-call(f32[4,184,256]{2,1,0:T(8,128)} %get-tuple-element.29.own, bf16[4,184,256]{2,1,0:T(8,128)(2,1)} %get-tuple-element.30.halo, bf16[32,32,128]{2,1,0:T(8,128)(2,1)} %get-tuple-element.31.g), custom_call_target="tpu_custom_call" | custom-call | tf_op jit(solution)/shard_map/reduce/pallas_call | solution.py:412
  44.3 4.1 %finish.1 = (f32[736,256]{1,0:T(8,128)}, f32[256,128]{1,0:T(8,128)}, f32[256,128]{1,0:T(8,128)}, f32[256,128]{1,0:T(8,128)}, f32[128,256]{1,0:T(8,128)}) custom-call(bf16[2,4,184,256]{3,2,1,0:T(8,128)(2,1)} %get-tuple-element.32.shares, bf16[32,32,128]{2,1,0:T(8,128)(2,1)} %get-tuple-element.33.ag, bf16[256,128]{1,0:T(8,128)(2,1)} %wk.3, bf16[256,128]{1,0:T(8,128)(2,1)} %wv.3), custom_call_target="tpu_custom_call" | custom-call | tf_op jit(solution)/shard_map/finish/pallas_call | solution.py:442

commit v4 on v3

--- a/solution.py
+++ b/solution.py
@@ -33,27 +33,7 @@
     return copy
 
 
-def live_rows(mask_ref, cnt, first, tiles, width):
-    length = mask_ref.shape[1]
-    row_id = lax.broadcasted_iota(jnp.int32, (length, width), 0)
-    blocks = []
-    for j in range(tiles):
-        t = first + j
-        used = jnp.sum(mask_ref[pl.ds(t, 1), :], axis=1, keepdims=True)
-        used = jnp.where(t < cnt[0], used, 0)
-        blocks.append((row_id < used).astype(F32))
-    return jnp.concatenate(blocks, axis=0)
-
-
-def halo_kernel(
-    n_inst, n_lon, parts, group, lat, x_hbm, cot_hbm, mask_ref, cnt, wq, wo,
-    low, high, q_hbm, g_hbm, x_ref, cot_ref, q_ref, g_ref,
-    send_sem, recv_sem, fan_send, fan_recv, load, store,
-):
-    loads = [pltpu.make_async_copy(x_hbm, x_ref, load.at[0]),
-             pltpu.make_async_copy(cot_hbm, cot_ref, load.at[1])]
-    for copy in loads:
-        copy.start()
+def halo_kernel(n_inst, n_lon, parts, lat, low, high, send_sem, recv_sem, fan_send, fan_recv):
     me, mi = lax.axis_index("lon"), lax.axis_index("inst")
     right, left = lax.rem(me + 1, n_lon), lax.rem(me + n_lon - 1, n_lon)
     peers = [lax.rem(mi + d, n_inst) for d in range(1, n_inst)] if parts > 1 else []
@@ -66,21 +46,6 @@
     mine = mi if parts > 1 else 0
     first = send(lat.at[parts + mine], low.at[mine], send_sem.at[0], recv_sem.at[0], {"lon": right})
     second = send(lat.at[mine], high.at[mine], send_sem.at[1], recv_sem.at[1], {"lon": left})
-    for copy in loads:
-        copy.wait()
-    n_tiles, length, width = x_ref.shape
-    for k in range(0, n_tiles, group):
-        at = pl.ds(k, group)
-        shape = (group, length, q_ref.shape[2])
-        flat = x_ref[at].reshape(group * length, width)
-        q_ref[at] = dot(flat, wq[...]).astype(BF16).reshape(shape)
-        live = live_rows(mask_ref, cnt, k, group, width)
-        masked = (cot_ref[at].reshape(group * length, width).astype(F32) * live).astype(BF16)
-        g_ref[at] = dot(masked, wo[...], NT).astype(BF16).reshape(shape)
-    stores = [pltpu.make_async_copy(q_ref, q_hbm, store.at[0]),
-              pltpu.make_async_copy(g_ref, g_hbm, store.at[1])]
-    for copy in stores:
-        copy.start()
     fans = []
     for side, (copy, block) in enumerate(((first, low), (second, high))):
         copy.wait_recv()
@@ -90,12 +55,12 @@
                 {"inst": other}))
     first.wait_send()
     second.wait_send()
-    for copy in fans + stores:
+    for copy in fans:
         copy.wait()
 
 
 def attend_kernel(
-    lon_cols, lat_rows, tw, cnt, x_ref, cot_ref, q_ref, g_ref, mask_ref, lat, low, high, wq, wk, wv, wo,
+    lon_cols, lat_rows, tw, cnt, x_ref, cot_ref, mask_ref, lat, low, high, wq, wk, wv, wo,
     dec, og, own_out, halo_out, g_out, keys, values, kg, vg, qg, outg,
 ):
     step = pl.program_id(0)
@@ -128,8 +93,18 @@
 
     flat_x = x_ref[...].reshape(tiles * length, width)
     flat_cot = cot_ref[...].reshape(tiles * length, width)
-    live = live_rows(mask_ref, cnt, step * tiles, tiles, width)
+    queries = dot(flat_x, wq[...]).astype(BF16)
+
+    row_id = lax.broadcasted_iota(jnp.int32, (length, width), 0)
+    lives = []
+    for j in range(tiles):
+        t = step * tiles + j
+        used = jnp.sum(mask_ref[pl.ds(t, 1), :], axis=1, keepdims=True)
+        used = jnp.where(t < cnt[0], used, 0)
+        lives.append(row_id < used)
+    live = jnp.concatenate([m.astype(F32) for m in lives], axis=0)
     masked = (flat_cot.astype(F32) * live).astype(BF16)
+    att_grad = dot(masked, wo[...], NT).astype(BF16)
 
     lane = lax.broadcasted_iota(jnp.int32, (1, attn), 1) // head
     head_mask = [(lane == h).astype(F32) for h in range(HEADS)]
@@ -142,8 +117,8 @@
         t = step * tiles + j
         col = lax.rem(tw[0, t] - band_first + REACH + lon_cols, lon_cols)
         base = col * lat_rows + tw[1, t]
-        q_t = q_ref[j]
-        g_t = g_ref[j]
+        q_t = queries[j * length : (j + 1) * length]
+        g_t = att_grad[j * length : (j + 1) * length]
         spans = [pl.ds(base + a * lat_rows, SUB) for a in range(WINDOW)]
         kw = jnp.concatenate([keys[at, :] for at in spans], axis=0)
         vw = jnp.concatenate([values[at, :] for at in spans], axis=0)
@@ -180,7 +155,7 @@
         parts = own_out.shape[0] // 2
         for ref, lanes in ((kg, pl.ds(0, attn)), (vg, pl.ds(attn, attn))):
             for k in range(2 * parts):
-                own_out[k, :, lanes] = ref[pl.ds(edge + k * half, half), :]
+                own_out[k, :, lanes] = ref[pl.ds(edge + k * half, half), :].astype(BF16)
                 at = k * half if k < parts else own_rows + k * half
                 halo_out[k, :, lanes] = ref[pl.ds(at, half), :].astype(BF16)
         kv = jnp.zeros((width, 2 * attn), F32)
@@ -200,7 +175,7 @@
 
 
 def reduce_kernel(
-    n_inst, n_lon, parts, gp, own, halo, g, shares, ag,
+    n_inst, n_lon, parts, gp, own_hbm, halo_hbm, g_hbm, shares, ag, own, halo, g, load,
     pre, hsum, hbuf, share, rs, part, mine, gpre, gsum, b_s, b_r, h_s, h_r, i_s, i_r, rs_s, rs_r,
     p_s, p_r, a_s, a_r, f_s, f_r, local,
 ):
@@ -213,6 +188,12 @@
     def inst_at(d):
         return lax.rem(mi + d, n_inst)
 
+    loads = [
+        pltpu.make_async_copy(src, dst, load.at[k])
+        for k, (src, dst) in enumerate(((g_hbm, g), (halo_hbm, halo), (own_hbm, own)))
+    ]
+    for copy in loads:
+        copy.start()
     barrier = pltpu.get_barrier_semaphore()
     for d in range(1, n_lon):
         pl.semaphore_signal(barrier, inc=1, device_id={"lon": lon_at(d)}, device_id_type=MESH)
@@ -220,6 +201,8 @@
         pl.semaphore_signal(barrier, inc=1, device_id={"inst": inst_at(d)}, device_id_type=MESH)
     pl.semaphore_wait(barrier, n_lon + n_inst - 2)
 
+    for copy in loads:
+        copy.wait()
     joined, presums = [], []
     if gp > 1:
         presums = [
@@ -259,7 +242,7 @@
         halos.append(send(
             hsum.at[side], hbuf.at[side], h_s.at[side], h_r.at[side], {"lon": lon_at(d)}))
     for k in range(2 * parts):
-        share[k] = own[k].astype(BF16)
+        share[k] = own[k]
     for copy in scatters:
         copy.wait()
     total = source[me].astype(F32)
@@ -292,8 +275,8 @@
     keep.start()
     for copy in halos:
         copy.wait()
-    share[slot] = (own[slot] + hbuf[1].astype(F32)).astype(BF16)
-    share[parts + slot] = (own[parts + slot] + hbuf[0].astype(F32)).astype(BF16)
+    share[slot] = (own[slot].astype(F32) + hbuf[1].astype(F32)).astype(BF16)
+    share[parts + slot] = (own[parts + slot].astype(F32) + hbuf[0].astype(F32)).astype(BF16)
     joins = [
         send(share, shares.at[mi], i_s.at[d], i_r.at[d], {"inst": inst_at(d)})
         for d in range(1, n_inst)
@@ -313,7 +296,7 @@
         copy.wait()
 
 
-def finish_kernel(shares, ag, wk, wv, lat_out, q_out, k_out, v_out, o_out):
+def finish_kernel(lat_rows, shares, ag, wk, wv, lat_out, q_out, k_out, v_out, o_out):
     attn = wk.shape[1]
     grad = shares[0, 0].astype(F32)
     for i in range(1, shares.shape[0]):
@@ -323,15 +306,14 @@
     w_pair = jnp.concatenate([wk[...], wv[...]], axis=1)
     lat_out[...] = dot(grad_high, w_pair, NT) + dot(grad_low, w_pair, NT)
 
-    @pl.when(pl.program_id(0) == 0)
-    def _():
-        rows = ag.shape[1]
-        at = 0
-        out_parts = [o_out.at[:, pl.ds(0, attn)], o_out.at[:, pl.ds(attn, attn)]]
-        for out in [q_out, k_out, v_out] + out_parts:
-            count = out.shape[0] // rows
-            out[...] = ag[pl.ds(at, count)].astype(F32).reshape(out.shape)
-            at += count
+    rows = ag.shape[1]
+    step, steps = pl.program_id(0), lat_rows // lat_out.shape[0]
+    at = 0
+    out_parts = [o_out.at[:, pl.ds(0, attn)], o_out.at[:, pl.ds(attn, attn)]]
+    for out in [q_out, k_out, v_out] + out_parts:
+        count = out.shape[0] // rows
+        out[...] = ag[pl.ds(at + step * count, count)].astype(F32).reshape(out.shape)
+        at += steps * count
 
 
 def vmem():
@@ -354,28 +336,21 @@
     anywhere = pl.BlockSpec(memory_space=pl.ANY)
     group = next(b for b in (4, 3, 2, 1) if n_tiles % b == 0)
     smem = pl.BlockSpec(memory_space=pltpu.SMEM)
-    low, high, queries, att_grad = pl.pallas_call(
-        functools.partial(halo_kernel, n_inst, n_lon, parts, group),
-        out_shape=[jax.ShapeDtypeStruct((parts, half, width), BF16)] * 2
-        + [jax.ShapeDtypeStruct((n_tiles, length, attn), BF16)] * 2,
-        in_specs=[anywhere] * 3 + [vmem(), smem, vmem(), vmem()],
-        out_specs=[anywhere] * 4,
-        scratch_shapes=[
-            pltpu.VMEM(obs_x.shape, BF16), pltpu.VMEM(obs_x.shape, BF16),
-            pltpu.VMEM((n_tiles, length, attn), BF16), pltpu.VMEM((n_tiles, length, attn), BF16),
-            dma((2,)), dma((2,)), dma((2, n_inst)), dma((2, n_inst)), dma((2,)), dma((2,)),
-        ],
+    low, high = pl.pallas_call(
+        functools.partial(halo_kernel, n_inst, n_lon, parts),
+        out_shape=[jax.ShapeDtypeStruct((parts, half, width), BF16)] * 2,
+        in_specs=[anywhere],
+        out_specs=[anywhere] * 2,
+        scratch_shapes=[dma((2,)), dma((2,)), dma((2, n_inst)), dma((2, n_inst))],
         compiler_params=pltpu.CompilerParams(collective_id=0, has_side_effects=True),
         name="halo",
-    )(latents.reshape(2 * parts, half, width), obs_x, obs_cot, point_mask, band_counts,
-      w_query, w_out)
+    )(latents.reshape(2 * parts, half, width))
     low, high = low.reshape(edge, width), high.reshape(edge, width)
 
     weight_rows = 2 * width + 2 * attn + width
     rows = weight_rows // n_lon
     gp = n_inst if rows % (2 * SUB * n_inst) == 0 else 1
     rows = rows // gp
-    head_spec = pl.BlockSpec((group, length, attn), lambda i: (i, 0, 0))
     whole = lambda *shape: pl.BlockSpec(shape, lambda i: (0,) * len(shape))
     tile_spec = pl.BlockSpec((group, length, width), lambda i: (i, 0, 0))
     decoded, obs_grad, own, halo, g = pl.pallas_call(
@@ -384,12 +359,12 @@
         out_shape=[
             jax.ShapeDtypeStruct(obs_x.shape, BF16),
             jax.ShapeDtypeStruct(obs_x.shape, BF16),
-            jax.ShapeDtypeStruct((2 * parts, half, 2 * attn), F32),
+            jax.ShapeDtypeStruct((2 * parts, half, 2 * attn), BF16),
             jax.ShapeDtypeStruct((2 * parts, half, 2 * attn), BF16),
             jax.ShapeDtypeStruct((gp * n_lon, rows, attn), BF16),
         ],
         in_specs=[
-            smem, smem, tile_spec, tile_spec, head_spec, head_spec, whole(n_tiles, length), whole(own_rows, width),
+            smem, smem, tile_spec, tile_spec, whole(n_tiles, length), whole(own_rows, width),
             whole(edge, width), whole(edge, width), whole(width, attn), whole(width, attn),
             whole(width, attn), whole(attn, width),
         ],
@@ -406,7 +381,7 @@
             pltpu.VMEM((attn, width), F32),
         ],
         name="attend",
-    )(tile_window.T, band_counts, obs_x, obs_cot, queries, att_grad, point_mask, flat, low, high,
+    )(tile_window.T, band_counts, obs_x, obs_cot, point_mask, flat, low, high,
       w_query, w_key, w_value, w_out)
 
     shares, ag = pl.pallas_call(
@@ -415,9 +390,13 @@
             jax.ShapeDtypeStruct((n_inst, 2 * parts, half, 2 * attn), BF16),
             jax.ShapeDtypeStruct((gp * n_lon, rows, attn), BF16),
         ],
-        in_specs=[vmem()] * 3,
+        in_specs=[anywhere] * 3,
         out_specs=[anywhere] * 2,
         scratch_shapes=[
+            pltpu.VMEM((2 * parts, half, 2 * attn), BF16),
+            pltpu.VMEM((2 * parts, half, 2 * attn), BF16),
+            pltpu.VMEM((gp * n_lon, rows, attn), BF16),
+            dma((3,)),
             pltpu.VMEM((2, n_inst, half, 2 * attn), BF16),
             pltpu.VMEM((2, half, 2 * attn), BF16),
             pltpu.VMEM((2, half, 2 * attn), BF16),
@@ -440,7 +419,7 @@
         name="reduce",
     )(own, halo, g)
     latent_grad, query_grad, key_grad, value_grad, out_grad = pl.pallas_call(
-        finish_kernel,
+        functools.partial(finish_kernel, own_rows),
         grid=(2 * parts,),
         out_shape=[
             jax.ShapeDtypeStruct((own_rows, width), F32),
@@ -454,8 +433,9 @@
             whole(gp * n_lon, rows, attn), whole(width, attn), whole(width, attn),
         ],
         out_specs=[
-            pl.BlockSpec((half, width), lambda i: (i, 0)), whole(width, attn),
-            whole(width, attn), whole(width, attn), whole(attn, width),
+            pl.BlockSpec((half, width), lambda i: (i, 0)),
+            *[pl.BlockSpec((width // (2 * parts), attn), lambda i: (i, 0))] * 3,
+            pl.BlockSpec((attn // (2 * parts), width), lambda i: (i, 0)),
         ],
         name="finish",
     )(shares, ag, w_key, w_value)

time: 48.7 us -> 46.3 us (0.951)
  Pallas kernels: 47.1 us -> 44.8 us
    pallas_call x1, Pallas kernels: 20.8 us -> 19.5 us  [shards(): pl.pallas_call(functools.partial(reduce_kernel, n_inst, n_lon, parts, gp)...]
    pallas_call x2, Pallas kernels: 17.2 us -> 16.2 us  [the longest x1 12.2 us: shards(): pl.pallas_call(functools.partial(halo_kernel, n_inst, n_lon, parts), out_...]
where the time goes in v4:
time: 46.3 us; the launch traced here: 46.1 us
  Pallas kernels  44.8 us (97%)
  between operations  1.3 us (3%)
    pallas_call x1, Pallas kernels, shards(): pl.pallas_call(functools.partial(reduce_kernel, n_inst, n_lon, parts, gp)...  19.5 us
    pallas_call x1, Pallas kernels, shards(): pl.pallas_call(functools.partial(halo_kernel, n_inst, n_lon, parts), out_...  12.2 us
    pallas_call x1, Pallas kernels, shards(): pl.pallas_call(functools.partial(attend_kernel, band_cols * n_lon, lat_ro...  9.1 us
    pallas_call x1, Pallas kernels, shards(): pl.pallas_call(functools.partial(finish_kernel, own_rows), grid=(2 * part...  3.95 us

profile of v4, /device:TPU:0, one launch (start us, length us, event | category | flops | bytes accessed | tf_op | source)
XLA Modules:
  0.0 46.1 jit_solution(16594849921677991628)
XLA Ops:
  1.3 12.2 %halo.1 = (bf16[2,184,256]{2,1,0:T(8,128)(2,1)}, bf16[2,184,256]{2,1,0:T(8,128)(2,1)}) custom-call(bf16[4,184,256]{2,1,0:T(8,128)(2,1)} %lat.1), custom_call_target="tpu_custom_call" | custom-call | tf_op jit(solution)/shard_map/halo/pallas_call | solution.py:339
  13.5 9.1 %attend.1 = (bf16[12,128,256]{2,1,0:T(8,128)(2,1)}, bf16[12,128,256]{2,1,0:T(8,128)(2,1)}, bf16[4,184,256]{2,1,0:T(8,128)(2,1)}, bf16[4,184,256]{2,1,0:T(8,128)(2,1)}, bf16[32,32,128]{2,1,0:T(8,128)(2,1)}) custom-call(s32[2,12]{1,0:T(2,128)} %bitcast.8, s32[1]{0:T(128)S(6)} %copy.17.cnt, bf16[12,128,256]{2,1,0:T(8,128)(2,1)} %x_ref.1, ...), custom_call_target="tpu_custom_call" | custom-call | tf_op jit(solution)/shard_map/attend/pallas_call | solution.py:356
  22.6 19.5 %reduce.1 = (bf16[2,4,184,256]{3,2,1,0:T(8,128)(2,1)}, bf16[32,32,128]{2,1,0:T(8,128)(2,1)}) custom-call(bf16[4,184,256]{2,1,0:T(8,128)(2,1)} %get-tuple-element.25.own_hbm, bf16[4,184,256]{2,1,0:T(8,128)(2,1)} %get-tuple-element.26.halo_hbm, bf16[32,32,128]{2,1,0:T(8,128)(2,1)} %get-tuple-element.27.g_hbm), custom_call_target="tpu_custom_call" | custom-call | tf_op jit(solution)/shard_map/reduce/pallas_call | solution.py:387
  42.1 4.0 %finish.1 = (f32[736,256]{1,0:T(8,128)}, f32[256,128]{1,0:T(8,128)}, f32[256,128]{1,0:T(8,128)}, f32[256,128]{1,0:T(8,128)}, f32[128,256]{1,0:T(8,128)}) custom-call(bf16[2,4,184,256]{3,2,1,0:T(8,128)(2,1)} %get-tuple-element.28.shares, bf16[32,32,128]{2,1,0:T(8,128)(2,1)} %get-tuple-element.29.ag, bf16[256,128]{1,0:T(8,128)(2,1)} %wk.3, bf16[256,128]{1,0:T(8,128)(2,1)} %wv.3), custom_call_target="tpu_custom_call" | custom-call | tf_op jit(solution)/shard_map/finish/pallas_call | solution.py:421
